TPU v7x, 32 devices: a whole 2x2x4 slice. The times are simulated.
32 devices in a mesh: dp: 16 (over z, y, core), ctx: 2 (over x).
Axes of the slice: x: 2, y: 2, z: 4, core: 2. Of those that a mesh axis runs over, the one named last changes fastest.
Arguments:
- tokens: bfloat16 [32, 1024, 1024], P('dp', 'ctx'), may hold values from -6 to 6
- cotangent: bfloat16 [32, 1024, 1024], P('dp', 'ctx'), may hold values from -6 to 6
- w_qkv: bfloat16 [1024, 3072], P(('dp', 'ctx')), may hold values from -0.1875 to 0.1875
- w_out: bfloat16 [1024, 1024], P(('dp', 'ctx')), may hold values from -3 to 3
- w_gate: bfloat16 [1024, 2624], P(('dp', 'ctx')), may hold values from -0.1875 to 0.1875
- w_up: bfloat16 [1024, 2624], P(('dp', 'ctx')), may hold values from -0.1875 to 0.1875
- w_down: bfloat16 [2624, 1024], P(None, ('dp', 'ctx')), may hold values from -0.125 to 0.125
- gain_one: bfloat16 [1024], P(('dp', 'ctx')), may hold values from 0.099609375 to 1.8984375
- gain_two: bfloat16 [1024], P(('dp', 'ctx')), may hold values from 0.099609375 to 1.8984375
Outputs:
- result: bfloat16 [32, 1024, 1024], P('dp', 'ctx')
- input_grad: bfloat16 [32, 1024, 1024], P('dp', 'ctx')
- grad_qkv: float32 [1024, 3072], P(('dp', 'ctx'))
- grad_out: float32 [1024, 1024], P(('dp', 'ctx'))
- grad_gate: float32 [1024, 2624], P(('dp', 'ctx'))
- grad_up: float32 [1024, 2624], P(('dp', 'ctx'))
- grad_down: float32 [2624, 1024], P(None, ('dp', 'ctx'))
- grad_gain_one: float32 [1024], P(('dp', 'ctx'))
- grad_gain_two: float32 [1024], P(('dp', 'ctx'))
All inputs are finite; a program needn't handle non-finite values.
Results may differ from a plain program's by a relative error of at most 0.025.
Values may be sent and summed in bfloat16 or wider, within the bound.
No kernel may reach another device: no remote copies, remote signals or barrier semaphores. Data moves between devices by JAX's collectives and lax.ppermute only.
A program may use at most 448 MiB of HBM per device.

v0:
```python
import math

import jax
import jax.numpy as jnp
from jax import lax
from jax.sharding import PartitionSpec as P

HEADS = 16
HEAD_DIM = 64


THETA = 160000.0
EPSILON = 1e-05


def rotary_tables(length, offset, head_size):
    halfway = head_size // 2
    frequency = jnp.exp(
        jnp.arange(halfway).astype(jnp.float32) * (-2.0 * math.log(THETA) / head_size)
    )
    position = (offset + jnp.arange(length)).astype(jnp.float32)
    angles = position[:, None] * frequency[None, :]
    cosine = jnp.cos(angles)
    sine_table = jnp.sin(angles)
    return (jnp.concatenate([cosine, cosine], -1), jnp.concatenate([sine_table, sine_table], -1))


def rotate_half(values):
    halfway = values.shape[-1] // 2
    return jnp.concatenate([-values[..., halfway:], values[..., :halfway]], -1)


def turn(values, cosine, sine_table):
    return values * cosine[:, None, :] + rotate_half(values) * sine_table[:, None, :]


def unturn(values, cosine, sine_table):
    return values * cosine[:, None, :] - rotate_half(values) * sine_table[:, None, :]


def standardize(values):
    centered = values - jnp.mean(values, -1, keepdims=True)
    inverse = lax.rsqrt(jnp.mean(centered * centered, -1, keepdims=True) + EPSILON)
    return (centered * inverse, inverse)


def norm_back(grad_normed, normed, inverse, gain_full):
    scaled = grad_normed * gain_full
    inner = (
        scaled
        - jnp.mean(scaled, -1, keepdims=True)
        - normed * jnp.mean(scaled * normed, -1, keepdims=True)
    )
    return (inverse * inner, jnp.sum(grad_normed * normed, 0))


def against(left, weight):
    return lax.dot_general(
        left, weight, (((1,), (1,)), ((), ())), preferred_element_type=jnp.float32
    )


def outer_sum(left, right):
    return lax.dot_general(
        left, right, (((0,), (0,)), ((), ())), preferred_element_type=jnp.float32
    )


def body(tokens, cotangent, w_qkv, w_out, w_gate, w_up, w_down, gain_one, gain_two):
    members, local_len, width = tokens.shape
    rows = members * local_len
    shards = (w_qkv, w_out, w_gate, w_up, w_down, gain_one, gain_two)
    offset = lax.axis_index("ctx") * local_len
    cosine, sine_table = rotary_tables(local_len, offset, HEAD_DIM)
    current = (
        lax.all_gather(shards[0], ("dp", "ctx"), axis=0, tiled=True),
        lax.all_gather(shards[1], ("dp", "ctx"), axis=0, tiled=True),
        lax.all_gather(shards[2], ("dp", "ctx"), axis=0, tiled=True),
        lax.all_gather(shards[3], ("dp", "ctx"), axis=0, tiled=True),
        lax.all_gather(shards[4], ("dp", "ctx"), axis=1, tiled=True),
        lax.all_gather(shards[5], ("dp", "ctx"), axis=0, tiled=True),
        lax.all_gather(shards[6], ("dp", "ctx"), axis=0, tiled=True),
    )
    full_qkv, full_out, full_gate, full_up, full_down, full_one, full_two = current
    inputs_f = tokens.astype(jnp.float32).reshape(rows, width)
    normed_one, inverse_one = standardize(inputs_f)
    first = (normed_one * full_one.astype(jnp.float32)).astype(jnp.bfloat16)
    merged = jnp.dot(first, full_qkv, preferred_element_type=jnp.float32)
    queries = turn(
        merged[:, :width].reshape(members, local_len, HEADS, HEAD_DIM), cosine, sine_table
    ).astype(jnp.bfloat16)
    key_own = turn(
        merged[:, width : 2 * width].reshape(members, local_len, HEADS, HEAD_DIM),
        cosine,
        sine_table,
    ).astype(jnp.bfloat16)
    value_own = (
        merged[:, 2 * width :].astype(jnp.bfloat16).reshape(members, local_len, HEADS, HEAD_DIM)
    )
    key_all, value_all = (
        lax.all_gather(key_own.reshape(members, local_len, width), "ctx", axis=1, tiled=True),
        lax.all_gather(value_own.reshape(members, local_len, width), "ctx", axis=1, tiled=True),
    )
    full_len = key_all.shape[1]
    key_heads = key_all.reshape(members, full_len, HEADS, HEAD_DIM)
    value_heads = value_all.reshape(members, full_len, HEADS, HEAD_DIM)
    scores = (
        jnp.einsum("bqhd,bkhd->bhqk", queries, key_heads, preferred_element_type=jnp.float32)
        * 0.125
    )
    peak = jnp.max(scores, -1, keepdims=True)
    log_total = peak + jnp.log(jnp.sum(jnp.exp(scores - peak), -1, keepdims=True))
    probs = jnp.exp(scores - log_total)
    attended = jnp.einsum(
        "bhqk,bkhd->bqhd",
        probs.astype(jnp.bfloat16),
        value_heads,
        preferred_element_type=jnp.float32,
    )
    attended = attended.reshape(rows, width).astype(jnp.bfloat16)
    residual = inputs_f + jnp.dot(attended, full_out, preferred_element_type=jnp.float32)
    normed_two, inverse_two = standardize(residual)
    second = (normed_two * full_two.astype(jnp.float32)).astype(jnp.bfloat16)
    gate_val = jnp.dot(second, full_gate, preferred_element_type=jnp.float32)
    up_val = jnp.dot(second, full_up, preferred_element_type=jnp.float32)
    hidden = (jax.nn.gelu(gate_val, approximate=False) * up_val).astype(jnp.bfloat16)
    outcome = residual + jnp.dot(hidden, full_down, preferred_element_type=jnp.float32)
    grad_top = cotangent.astype(jnp.float32).reshape(rows, width)
    grad_low = grad_top.astype(jnp.bfloat16)
    grad_hidden = against(grad_low, full_down)
    activated, gelu_pull = jax.vjp(
        lambda pre_act: jax.nn.gelu(pre_act, approximate=False), gate_val
    )
    grad_gate = gelu_pull(grad_hidden * up_val)[0].astype(jnp.bfloat16)
    grad_up = (grad_hidden * activated).astype(jnp.bfloat16)
    grad_second = against(grad_gate, full_gate) + against(grad_up, full_up)
    grad_resid, part_two = norm_back(
        grad_second, normed_two, inverse_two, full_two.astype(jnp.float32)
    )
    grad_resid = grad_resid + grad_top
    grad_proj = grad_resid.astype(jnp.bfloat16)
    grad_att = (
        against(grad_proj, full_out)
        .astype(jnp.bfloat16)
        .reshape(members, local_len, HEADS, HEAD_DIM)
    )
    scores = (
        jnp.einsum("bqhd,bkhd->bhqk", queries, key_heads, preferred_element_type=jnp.float32)
        * 0.125
    )
    probs = jnp.exp(scores - log_total)
    grad_probs = jnp.einsum(
        "bqhd,bkhd->bhqk", grad_att, value_heads, preferred_element_type=jnp.float32
    )
    row_delta = jnp.sum(grad_probs * probs, -1, keepdims=True)
    grad_scores = (probs * (grad_probs - row_delta)).astype(jnp.bfloat16)
    grad_query = (
        jnp.einsum("bhqk,bkhd->bqhd", grad_scores, key_heads, preferred_element_type=jnp.float32)
        * 0.125
    )
    value_terms = jnp.einsum(
        "bhqk,bqhd->bkhd", probs.astype(jnp.bfloat16), grad_att, preferred_element_type=jnp.float32
    )
    key_terms = (
        jnp.einsum("bhqk,bqhd->bkhd", grad_scores, queries, preferred_element_type=jnp.float32)
        * 0.125
    )
    grad_key, grad_value = (
        lax.psum_scatter(
            key_terms.reshape(members, full_len, width).astype(jnp.bfloat16),
            "ctx",
            scatter_dimension=1,
            tiled=True,
        ).astype(jnp.float32),
        lax.psum_scatter(
            value_terms.reshape(members, full_len, width).astype(jnp.bfloat16),
            "ctx",
            scatter_dimension=1,
            tiled=True,
        ).astype(jnp.float32),
    )
    grad_key = grad_key.reshape(rows, width)
    grad_value = grad_value.reshape(rows, width)
    query_pre = unturn(grad_query, cosine, sine_table).reshape(rows, width)
    key_pre = unturn(
        grad_key.reshape(members, local_len, HEADS, HEAD_DIM), cosine, sine_table
    ).reshape(rows, width)
    grad_merged = jnp.concatenate([query_pre, key_pre, grad_value], 1).astype(jnp.bfloat16)
    grad_first = against(grad_merged, full_qkv)
    grad_in, part_one = norm_back(grad_first, normed_one, inverse_one, full_one.astype(jnp.float32))
    input_grad = (grad_in + grad_resid).astype(jnp.bfloat16).reshape(members, local_len, width)
    local_grads = (
        outer_sum(first, grad_merged),
        outer_sum(attended, grad_proj),
        outer_sum(second, grad_gate),
        outer_sum(second, grad_up),
        outer_sum(grad_low, hidden),
        part_one,
        part_two,
    )
    shares = (
        lax.psum_scatter(local_grads[0], ("dp", "ctx"), scatter_dimension=0, tiled=True),
        lax.psum_scatter(local_grads[1], ("dp", "ctx"), scatter_dimension=0, tiled=True),
        lax.psum_scatter(local_grads[2], ("dp", "ctx"), scatter_dimension=0, tiled=True),
        lax.psum_scatter(local_grads[3], ("dp", "ctx"), scatter_dimension=0, tiled=True),
        lax.psum_scatter(local_grads[4], ("dp", "ctx"), scatter_dimension=0, tiled=True),
        lax.psum_scatter(local_grads[5], ("dp", "ctx"), scatter_dimension=0, tiled=True),
        lax.psum_scatter(local_grads[6], ("dp", "ctx"), scatter_dimension=0, tiled=True),
    )
    return (
        outcome.astype(jnp.bfloat16).reshape(members, local_len, width),
        input_grad,
        shares[0],
        shares[1],
        shares[2],
        shares[3],
        shares[4].T,
        shares[5],
        shares[6],
    )


def solution(mesh):
    in_specs = (
        P("dp", "ctx", None),
        P("dp", "ctx", None),
        P(("dp", "ctx"), None),
        P(("dp", "ctx"), None),
        P(("dp", "ctx"), None),
        P(("dp", "ctx"), None),
        P(None, ("dp", "ctx")),
        P(("dp", "ctx")),
        P(("dp", "ctx")),
    )
    out_specs = (
        P("dp", "ctx", None),
        P("dp", "ctx", None),
        P(("dp", "ctx"), None),
        P(("dp", "ctx"), None),
        P(("dp", "ctx"), None),
        P(("dp", "ctx"), None),
        P(None, ("dp", "ctx")),
        P(("dp", "ctx")),
        P(("dp", "ctx")),
    )
    return jax.shard_map(body, mesh=mesh, in_specs=in_specs, out_specs=out_specs, check_vma=False)
```

profile of v0, /device:TPU:0, one launch (start us, length us, event | category | flops | bytes accessed | tf_op | source)
XLA Modules:
  0.0 1538.5 jit_solution(12603042096230104438)
XLA Ops:
  9.7 43.1 %all-reduce.5 = (bf16[1024]{0:T(1024)(128)(2,1)S(1)}, bf16[1024]{0:T(1024)(128)(2,1)S(1)}) all-reduce(bf16[1024]{0:T(1024)(128)(2,1)S(1)} %dynamic-update-slice, bf16[1024]{0:T(1024)(128)(2,1)S(1)} %dynamic-update-slice.1), channel_id=1, replica_groups=mesh['dp'=16,'ctx'=2] {'dp','ctx'}, use_global_device_ids=true, to_apply=%add | all-reduce | flops 2048 | bytes 8192
  60.1 23.1 %all-gather.8.cloned.1.call-done = bf16[1024,3072]{1,0:T(8,128)(2,1)} async-done(((bf16[32,3072]{1,0:T(8,128)(2,1)}), bf16[1024,3072]{1,0:T(8,128)(2,1)}) %all-gather.8.cloned.1.call-update) | async-done | bytes 6291472 | tf_op jit(solution)/shard_map/all_gather | solution.py:76
  157.2 28.0 %all-gather.12.cloned.1.call-done = bf16[2,1024,1024]{1,2,0:T(8,128)(2,1)} async-done(((bf16[2,512,1024]{1,2,0:T(8,128)(2,1)}), bf16[2,1024,1024]{1,2,0:T(8,128)(2,1)}) %all-gather.12.cloned.1.call-update) | async-done | bytes 4194320 | tf_op jit(solution)/shard_map/all_gather | solution.py:101
  185.2 28.3 %multiply_reduce_fusion.1 = (f32[2,16,512]{2,1,0:T(8,128)S(1)}, f32[2,16,512,1024]{3,2,1,0:T(8,128)}) fusion(bf16[2,512,16,64]{1,3,2,0:T(8,128)(2,1)} %fusion.12, bf16[2,1024,16,64]{1,3,2,0:T(8,128)(2,1)} %bitcast.131), kind=kOutput, calls=%fused_computation.4 | convolution fusion | flops 2181021696 | bytes 73465856 | tf_op jit(solution)/shard_map/bqhd,bkhd->bhqk/dot_general | solution.py:108
  213.5 21.3 %exponential_reduce_fusion = f32[2,16,512]{2,1,0:T(8,128)S(1)} fusion(f32[2,16,512,1024]{3,2,1,0:T(8,128)} %get-tuple-element.69, f32[2,16,512]{2,1,0:T(8,128)S(1)} %get-tuple-element.68), kind=kLoop, calls=%fused_computation.3 | loop fusion | flops 50315264 | bytes 67239936 | tf_op jit(solution)/shard_map/reduce_sum | solution.py:112
  250.3 26.8 %convert_bitcast_fusion = bf16[2,512,16,64]{1,3,2,0:T(8,128)(2,1)} fusion(bf16[2,1024,16,64]{1,3,2,0:T(8,128)(2,1)} %bitcast.128, f32[2,16,512,1024]{3,2,1,0:T(8,128)} %get-tuple-element.69, f32[2,16,512]{2,1,0:T(8,128)S(1)} %log_add_fusion), kind=kOutput, calls=%fused_computation.79 | convolution fusion | flops 2198863872 | bytes 73465856 | tf_op jit(solution)/shard_map/bhqk,bkhd->bqhd/dot_general | solution.py:114
  282.8 20.6 %all-gather.14.cloned.1.call-done = bf16[1024,1024]{1,0:T(8,128)(2,1)} async-done(((bf16[32,1024]{1,0:T(8,128)(2,1)}), bf16[1024,1024]{1,0:T(8,128)(2,1)}) %all-gather.14.cloned.1.call-update) | async-done | bytes 2097168 | tf_op jit(solution)/shard_map/all_gather | solution.py:77
  312.6 58.7 %all-gather.16.cloned.1.call-done = bf16[1024,2624]{1,0:T(8,128)(2,1)} async-done(((bf16[32,2624]{1,0:T(8,128)(2,1)}), bf16[1024,2624]{1,0:T(8,128)(2,1)}) %all-gather.16.cloned.1.call-update) | async-done | bytes 5373968 | tf_op jit(solution)/shard_map/all_gather | solution.py:78
  382.6 56.4 %all-gather.20.cloned.1.call-done = bf16[2624,1024]{0,1:T(8,128)(2,1)} async-done(((bf16[2624,32]{0,1:T(8,128)(2,1)}), bf16[2624,1024]{0,1:T(8,128)(2,1)}) %all-gather.20.cloned.1.call-update) | async-done | bytes 5373968 | tf_op jit(solution)/shard_map/all_gather | solution.py:80
  439.0 33.4 %multiply_convert_fusion.1 = (bf16[1024,2624]{0,1:T(8,128)(2,1)}, f32[1024,2624]{0,1:T(8,128)}, f32[1024,2624]{0,1:T(8,128)}) fusion(f32[1024,2624]{0,1:T(8,128)} %fusion.50, bf16[1024,1024]{1,0:T(8,128)(2,1)S(1)} %bitcast.146, bf16[2624,1024]{0,1:T(8,128)(2,1)} %all-gather.20.cloned.1.call-done), kind=kOutput, calls=%fused_computation.8 | convolution fusion | flops 5680267264 | bytes 45088768 | tf_op jit(solution)/shard_map/dot_general | solution.py:58
  472.4 34.4 %all-gather.18.cloned.1.call-done = bf16[1024,2624]{1,0:T(8,128)(2,1)} async-done(((bf16[32,2624]{1,0:T(8,128)(2,1)}), bf16[1024,2624]{1,0:T(8,128)(2,1)}) %all-gather.18.cloned.1.call-update) | async-done | bytes 5373968 | tf_op jit(solution)/shard_map/all_gather | solution.py:79
  506.9 22.3 %add_convert_fusion = (bf16[1024,2624]{0,1:T(8,128)(2,1)}, bf16[1024,2624]{0,1:T(8,128)(2,1)}) fusion(f32[1024,2624]{0,1:T(8,128)} %get-tuple-element.47, f32[1024,2624]{0,1:T(8,128)} %get-tuple-element.72, f32[1024,2624]{0,1:T(8,128)} %fusion.50, bf16[1024,1024]{1,0:T(8,128)(2,1)} %multiply_convert_fusion.4, ...), kind=kOutput, calls=%fused_computation.9 | convolution fusion | flops 5551292416 | bytes 50462720 | tf_op jit(solution)/shard_map/dot_general | solution.py:125
  564.7 25.9 %fusion.31 = bf16[2,16,64,1024]{3,2,1,0:T(8,128)(2,1)} fusion(bf16[2,512,16,64]{1,3,2,0:T(8,128)(2,1)S(1)} %copy.59, f32[2,16,512,1024]{3,2,1,0:T(8,128)} %get-tuple-element.69, f32[2,16,512]{2,1,0:T(8,128)S(1)} %copy-done.15), kind=kOutput, calls=%fused_computation.72 | convolution fusion | flops 2199912448 | bytes 73465856 | tf_op jit(solution)/shard_map/bhqk,bqhd->bkhd/dot_general | solution.py:161
  590.6 48.5 %multiply_reduce_fusion = (f32[2,16,512]{2,1,0:T(8,128)S(1)}, f32[2,16,512,1024]{3,2,1,0:T(8,128)}) fusion(f32[2,16,512,1024]{3,2,1,0:T(8,128)} %get-tuple-element.69, f32[2,16,512]{2,1,0:T(8,128)S(1)} %copy-done.15, bf16[2,512,16,64]{1,3,2,0:T(8,128)(2,1)S(1)} %copy.59, bf16[2,1024,16,64]{1,3,2,0:T(8,128)(2,1)} %bitcast.129), kind=kOutput, calls=%fused_computation.1 | convolution fusion | flops 2214576128 | bytes 140640256 | tf_op jit(solution)/shard_map/bqhd,bkhd->bhqk/dot_general | solution.py:152
  645.4 54.6 %multiply_convert_fusion = bf16[2,16,512,1024]{3,2,1,0:T(8,128)(2,1)} fusion(f32[2,16,512,1024]{3,2,1,0:T(8,128)} %get-tuple-element.75, f32[2,16,512,1024]{3,2,1,0:T(8,128)} %get-tuple-element.69, f32[2,16,512]{2,1,0:T(8,128)S(1)} %get-tuple-element.74, f32[2,16,512]{2,1,0:T(8,128)S(1)} %copy-done.15), kind=kLoop, calls=%fused_computation | loop fusion | flops 83886080 | bytes 167903232 | tf_op jit(solution)/shard_map/convert_element_type | solution.py:156
  700.0 18.4 %multiply_convert_fusion.3 = bf16[2,16,64,1024]{3,2,1,0:T(8,128)(2,1)} fusion(bf16[2,512,16,64]{1,3,2,0:T(8,128)(2,1)S(1)} %copy-done.5, bf16[2,16,512,1024]{3,2,1,0:T(8,128)(2,1)} %multiply_convert_fusion), kind=kOutput, calls=%fused_computation.25 | convolution fusion | flops 2151677952 | bytes 39845888 | tf_op jit(solution)/shard_map/bhqk,bqhd->bkhd/dot_general | solution.py:165
  787.3 21.3 %bitcast_multiply_fusion = (f32[2,512,16,64]{1,3,2,0:T(8,128)}, f32[2,16,64,512]{3,2,1,0:T(8,128)}) fusion(bf16[2,1024,16,64]{1,3,2,0:T(8,128)(2,1)} %bitcast.132, bf16[2,16,512,1024]{3,2,1,0:T(8,128)(2,1)} %multiply_convert_fusion), kind=kOutput, calls=%fused_computation.39 | convolution fusion | flops 2148532224 | bytes 46137344 | tf_op jit(solution)/shard_map/bhqk,bkhd->bqhd/dot_general | solution.py:158
  851.9 13.7 fusion.34
  877.5 12.3 fusion.30
  889.9 39.8 %all-reduce.4 = (f32[1024]{0:T(1024)S(1)}, f32[1024]{0:T(1024)S(1)}) all-reduce(f32[1024]{0:T(1024)S(1)} %get-tuple-element.38, f32[1024]{0:T(1024)S(1)} %copy-done.44), channel_id=9, replica_groups=mesh['dp'=16,'ctx'=2] {'dp','ctx'}, use_global_device_ids=true, to_apply=%region_19.0.clone | all-reduce | flops 2048 | bytes 16384
  936.2 136.2 %reduce-scatter.20.cloned.1.call-done = f32[32,2624]{1,0:T(8,128)} async-done(((f32[1024,2624]{1,0:T(8,128)}), f32[32,2624]{1,0:T(8,128)}) %reduce-scatter.20.cloned.1.call-update) | async-done | bytes 335888 | tf_op jit(solution)/shard_map/reduce_scatter | solution.py:205
  1072.4 149.4 %reduce-scatter.18.cloned.1.call-done = f32[32,2624]{1,0:T(8,128)} async-done(((f32[1024,2624]{1,0:T(8,128)}), f32[32,2624]{1,0:T(8,128)}) %reduce-scatter.18.cloned.1.call-update) | async-done | bytes 335888 | tf_op jit(solution)/shard_map/reduce_scatter | solution.py:204
  1221.8 149.6 %reduce-scatter.22.cloned.1.call-done = f32[32,2624]{1,0:T(8,128)} async-done(((f32[1024,2624]{1,0:T(8,128)}), f32[32,2624]{1,0:T(8,128)}) %reduce-scatter.22.cloned.1.call-update) | async-done | bytes 335888
  1371.4 160.4 %reduce-scatter.14.cloned.1.call-done = f32[32,3072]{1,0:T(8,128)} async-done(((f32[1024,3072]{1,0:T(8,128)}), f32[32,3072]{1,0:T(8,128)}) %reduce-scatter.14.cloned.1.call-update) | async-done | bytes 393232 | tf_op jit(solution)/shard_map/reduce_scatter | solution.py:202
  (206 shorter events, 297.2 us)
Async XLA Ops:
  7.2 50.9 %copy-start.3 = (bf16[2,512,1024]{2,1,0:T(8,128)(2,1)S(1)}, bf16[2,512,1024]{2,1,0:T(8,128)(2,1)}, u32[]{:S(2)}) copy-start(bf16[2,512,1024]{2,1,0:T(8,128)(2,1)} %param.9) | copy-start | bytes 6291460
  7.2 76.0 %all-gather.8.cloned.1.call-start = ((), (), s32[]{:S(2)}) async-start(), calls=%async_computation.7 | async-start | bytes 6488064 | tf_op jit(solution)/shard_map/all_gather | solution.py:76
  7.9 177.3 %all-gather.12.cloned.1.call-start = ((), (), s32[]{:S(2)}) async-start(), calls=%async_computation.9 | async-start | bytes 6291456 | tf_op jit(solution)/shard_map/all_gather | solution.py:101
  54.7 37.9 %copy-start.36 = (f32[1,4,2,128]{3,1,2,0:T(4,128)}, f32[1,4,2,128]{3,1,2,0:T(4,128)S(1)}, u32[]{:S(2)}) copy-start(f32[1,4,2,128]{3,1,2,0:T(4,128)S(1)} %copy.79) | copy-start | bytes 12292
  57.0 35.6 %copy-start.38 = (f32[1,4,2,128]{3,1,2,0:T(4,128)}, f32[1,4,2,128]{3,1,2,0:T(4,128)S(1)}, u32[]{:S(2)}) copy-start(f32[1,4,2,128]{3,1,2,0:T(4,128)S(1)} %copy.80) | copy-start | bytes 12292
  58.1 96.3 %copy-start.16 = (f32[512,64]{0,1:T(8,128)}, f32[512,64]{0,1:T(8,128)S(1)}, u32[]{:S(2)}) copy-start(f32[512,64]{0,1:T(8,128)S(1)} %get-tuple-element.79) | copy-start | bytes 393220
  58.1 96.3 %copy-start.18 = (f32[512,64]{0,1:T(8,128)}, f32[512,64]{0,1:T(8,128)S(1)}, u32[]{:S(2)}) copy-start(f32[512,64]{0,1:T(8,128)S(1)} %get-tuple-element.63) | copy-start | bytes 393220
  129.9 114.3 %all-gather.10.cloned.1.call-start = ((), (), s32[]{:S(2)}) async-start(), calls=%async_computation.8 | async-start | bytes 6291456 | tf_op jit(solution)/shard_map/all_gather | solution.py:102
  133.8 169.6 %all-gather.14.cloned.1.call-start = ((), (), s32[]{:S(2)}) async-start(), calls=%async_computation.10 | async-start | bytes 2162688 | tf_op jit(solution)/shard_map/all_gather | solution.py:77
  134.3 236.9 %all-gather.16.cloned.1.call-start = ((), (), s32[]{:S(2)}) async-start(), calls=%async_computation.11 | async-start | bytes 5677056 | tf_op jit(solution)/shard_map/all_gather | solution.py:78
  134.9 304.1 %all-gather.20.cloned.1.call-start = ((), (), s32[]{:S(2)}) async-start(), calls=%async_computation.13 | async-start | bytes 5677056 | tf_op jit(solution)/shard_map/all_gather | solution.py:80
  135.5 371.4 %all-gather.18.cloned.1.call-start = ((), (), s32[]{:S(2)}) async-start(), calls=%async_computation.12 | async-start | bytes 5677056 | tf_op jit(solution)/shard_map/all_gather | solution.py:79
  136.3 676.6 %reduce-scatter.12.cloned.1.call-start = ((), (), s32[]{:S(2)}) async-start(), calls=%async_computation.15 | async-start | bytes 6291456 | tf_op jit(solution)/shard_map/reduce_scatter | solution.py:175
  136.3 172.4 %copy-start.40 = (f32[1024]{0:T(1024)}, f32[1024]{0:T(1024)S(1)}, u32[]{:S(2)}) copy-start(f32[1024]{0:T(1024)S(1)} %convert_element_type.112) | copy-start | bytes 12292
  312.6 126.4 %copy-start.20 = (bf16[2,512,1024]{2,1,0:T(8,128)(2,1)S(1)}, bf16[2,512,1024]{2,1,0:T(8,128)(2,1)}, u32[]{:S(2)}) copy-start(bf16[2,512,1024]{2,1,0:T(8,128)(2,1)} %param.10) | copy-start | bytes 6291460
  506.9 22.3 %copy-start.45 = (bf16[1024,2624]{1,0:T(8,128)(2,1)S(1)}, bf16[1024,2624]{1,0:T(8,128)(2,1)}, u32[]{:S(2)}) copy-start(bf16[1024,2624]{1,0:T(8,128)(2,1)} %all-gather.16.cloned.1.call-done) | copy-start | bytes 16121860
  645.4 171.4 %reduce-scatter.10.cloned.1.call-start = ((), (), s32[]{:S(2)}) async-start(), calls=%async_computation.14 | async-start | bytes 6291456 | tf_op jit(solution)/shard_map/reduce_scatter | solution.py:169
  645.4 54.6 %copy-start.5 = (bf16[2,512,16,64]{1,3,2,0:T(8,128)(2,1)S(1)}, bf16[2,512,16,64]{1,3,2,0:T(8,128)(2,1)}, u32[]{:S(2)}) copy-start(bf16[2,512,16,64]{1,3,2,0:T(8,128)(2,1)} %fusion.12) | copy-start | bytes 6291460
  724.7 211.5 %reduce-scatter.16.cloned.1.call-start = ((), (), s32[]{:S(2)}) async-start(), calls=%async_computation.17 | async-start | bytes 4325376 | tf_op jit(solution)/shard_map/reduce_scatter | solution.py:203
  732.7 339.7 %reduce-scatter.20.cloned.1.call-start = ((), (), s32[]{:S(2)}) async-start(), calls=%async_computation.19 | async-start | bytes 11354112 | tf_op jit(solution)/shard_map/reduce_scatter | solution.py:205
  745.9 476.0 %reduce-scatter.18.cloned.1.call-start = ((), (), s32[]{:S(2)}) async-start(), calls=%async_computation.18 | async-start | bytes 11354112 | tf_op jit(solution)/shard_map/reduce_scatter | solution.py:204
  757.3 614.1 %reduce-scatter.22.cloned.1.call-start = ((), (), s32[]{:S(2)}) async-start(), calls=%async_computation.20 | async-start | bytes 11354112
  781.8 750.0 %reduce-scatter.14.cloned.1.call-start = ((), (), s32[]{:S(2)}) async-start(), calls=%async_computation.16 | async-start | bytes 12976128 | tf_op jit(solution)/shard_map/reduce_scatter | solution.py:202
  831.3 19.4 %copy-start.29 = (bf16[128,8,2,512]{3,1,2,0:T(8,128)(2,1)}, bf16[128,8,2,512]{3,1,2,0:T(8,128)(2,1)S(1)}, u32[]{:S(2)}) copy-start(bf16[128,8,2,512]{3,1,2,0:T(8,128)(2,1)S(1)} %copy.82) | copy-start | bytes 6291460
  (38 other events, 233.4 us)
Sparse Core Ops, SparseCore 0:
  10.9 72.2 all-gather.7
  130.0 55.2 all-gather.11
  187.4 56.7 all-gather.9
  247.0 56.3 all-gather.13
  306.1 65.0 all-gather.15
  374.0 64.9 all-gather.19
  441.9 64.9 all-gather.17
  645.5 53.0 reduce-scatter.11
  724.8 53.3 reduce-scatter.9
  780.9 144.1 reduce-scatter.15
  931.6 140.8 reduce-scatter.19
  1078.8 142.9 reduce-scatter.17
  1228.4 142.9 reduce-scatter.21
  1377.9 153.8 reduce-scatter.13
where the time goes:
time: 1550 us; the launch traced here: 1540 us
  waiting for transfers between devices  829 us (53%)
  matrix products  351 us (23%)
  local copies, waits for them, and re-layouts  136 us (9%)
  other arithmetic  123 us (8%)
  blocking collectives  82.8 us (5%)
    reduce_scatter x1, waiting for transfers between devices, body(): lax.psum_scatter(local_grads[0], ('dp', 'ctx'), scatter_dimension=0, tile...  160 us
    unnamed x15, waiting for transfers between devices  153 us
    reduce_scatter x1, waiting for transfers between devices, body(): lax.psum_scatter(local_grads[2], ('dp', 'ctx'), scatter_dimension=0, tile...  149 us
    reduce_scatter x1, waiting for transfers between devices, body(): lax.psum_scatter(local_grads[3], ('dp', 'ctx'), scatter_dimension=0, tile...  136 us
    unnamed x2, blocking collectives  82.8 us
    dot_general x5, matrix products, against(): lax.dot_general(left, weight, (((1,), (1,)), ((), ())), preferred_element...  68.8 us
    all_gather x1, waiting for transfers between devices, body(): lax.all_gather(shards[2], ('dp', 'ctx'), axis=0, tiled=True)  58.7 us
    all_gather x1, waiting for transfers between devices, body(): lax.all_gather(shards[4], ('dp', 'ctx'), axis=1, tiled=True)  56.4 us
  transfers between devices with their start and end apart: 14, of which 11 were waited for; matrix products, arithmetic and copies ran while one was open for 27% of the time, Pallas kernels for 0%

commit v1 on v0

--- a/solution.py
+++ b/solution.py
@@ -1,8 +1,11 @@
+import functools
 import math
 
 import jax
 import jax.numpy as jnp
 from jax import lax
+from jax.experimental import pallas as pl
+from jax.experimental.pallas import tpu as pltpu
 from jax.sharding import PartitionSpec as P
 
 HEADS = 16
@@ -220,27 +223,555 @@
     )
 
 
+BF = jnp.bfloat16
+F32 = jnp.float32
+BITS = ("zh", "zl", "y", "c", "x")
+COORDS = pl.BlockSpec(memory_space=pltpu.SMEM)
+ANY = pl.BlockSpec(memory_space=pl.ANY)
+
+
+def swap(values, axis):
+    return lax.ppermute(values, axis, [(0, 1), (1, 0)])
+
+
+def nt(left, right):
+    return lax.dot_general(left, right, (((1,), (1,)), ((), ())), preferred_element_type=F32)
+
+
+def nn(left, right):
+    return jnp.dot(left, right, preferred_element_type=F32)
+
+
+def row_of(coords, zh, zl, y, c, x, half):
+    def bit(i, flip):
+        return coords[i] + flip - 2 * flip * coords[i]
+
+    top = (bit(0, zh) * 2 + bit(1, zl)) * 2 + bit(2, y)
+    row = ((top * 2 + bit(3, c)) * 2 + bit(4, x)) * 32 + half * 16
+    return pl.multiple_of(row, 16)
+
+
+class Chain:
+    def __init__(self, steps):
+        self.steps, self.value = steps, None
+        self.waiting = next(steps)
+
+    def go(self, *beside):
+        ready = self.waiting
+        if beside:
+            tied = lax.optimization_barrier((beside, ready))
+            beside, ready = tied
+        try:
+            self.waiting = self.steps.send(ready)
+        except StopIteration as stop:
+            self.value = stop.value
+        return beside[0] if len(beside) == 1 else beside
+
+
+def cost(micros):
+    return pl.CostEstimate(
+        flops=int(micros * 7e8), bytes_accessed=int(micros * 1e6), transcendentals=0
+    )
+
+
+def gather_steps(shard):
+    count, width = shard.shape
+    (parts,) = yield (shard.reshape(2, 16, width),)
+    (first,) = yield (jnp.stack([parts, swap(parts, "zh")]),)
+    other = swap(first, "zl")
+    blocks = yield tuple(
+        jnp.concatenate([first[:, half], other[:, half]], 0) for half in (0, 1)
+    )
+    a_x = swap(blocks[0], "x")
+    b_y = swap(blocks[1], "y")
+    a_two, b_two = yield (
+        jnp.concatenate([blocks[0], a_x], 0),
+        jnp.concatenate([blocks[1], b_y], 0),
+    )
+    mine = yield (a_two, swap(a_two, "y"), b_two, swap(b_two, "x"))
+    return tuple(mine) + tuple(swap(piece, "c") for piece in mine)
+
+
+def assemble_kernel(coords, *refs):
+    out = refs[8]
+    for index, piece in enumerate(refs[:8]):
+        c, kind = divmod(index, 4)
+        half, late = divmod(kind, 2)
+        for block in range(8):
+            pair, zl, zh = block // 4, (block // 2) % 2, block % 2
+            x, y = (pair, late) if half == 0 else (late, pair)
+            row = row_of(coords, zh, zl, y, c, x, half)
+            out[pl.ds(row, 16), :] = piece[block]
+
+
+def assemble(pieces, coords, width, block, start):
+    return pl.pallas_call(
+        assemble_kernel,
+        grid=(width // block,),
+        out_shape=jax.ShapeDtypeStruct((1024, width), BF),
+        in_specs=[COORDS] + [pl.BlockSpec((8, 16, block), lambda j: (0, 0, start + j))] * 8,
+        out_specs=pl.BlockSpec((1024, block), lambda j: (0, j)),
+        cost_estimate=cost(4),
+        name="assemble",
+    )(coords, *pieces)
+
+
+def grad_kernel(coords, x_ref, y_ref, *refs):
+    keep_ref, send_ref, xt_ref, acc_ref = refs[-4:]
+    j = pl.program_id(0)
+
+    @pl.when(j == 0)
+    def _():
+        for i in range(4):
+            rows = pl.ds(i * 256, 256)
+            xt_ref[:, rows] = x_ref[rows, :].astype(F32).T.astype(BF)
+
+    dy = y_ref[...]
+    acc_ref[...] = nn(xt_ref[...], dy.reshape(dy.shape[-2:]))
+    for c, out in ((0, keep_ref), (1, send_ref)):
+        for block in range(32):
+            half, a, b, zl, zh = [(block >> s) & 1 for s in (4, 3, 2, 1, 0)]
+            y, x = (a, b) if half == 0 else (b, a)
+            row = row_of(coords, zh, zl, y, c, x, half)
+            out[pl.ds(block * 16, 16), :] = acc_ref[pl.ds(row, 16), :].astype(BF)
+
+
+def grad_call(coords, left, right, right_spec, width, block, base, start, carry):
+    steps = width // block
+    out_spec = pl.BlockSpec((512, block), lambda j: (0, start + j))
+    operands = [coords, left, right]
+    in_specs = [COORDS, pl.BlockSpec((1024, 1024), lambda j: (0, 0)), right_spec]
+    aliases = {}
+    if carry is not None:
+        aliases = {len(operands): 0, len(operands) + 1: 1}
+        operands += list(carry)
+        in_specs += [ANY, ANY]
+    return pl.pallas_call(
+        grad_kernel,
+        grid=(steps,),
+        out_shape=[jax.ShapeDtypeStruct((512, base), BF)] * 2,
+        in_specs=in_specs,
+        out_specs=[out_spec, out_spec],
+        scratch_shapes=[pltpu.VMEM((1024, 1024), BF), pltpu.VMEM((1024, block), F32)],
+        input_output_aliases=aliases,
+        cost_estimate=cost(width / 230),
+        name="weight_grad",
+    )(*operands)
+
+
+def plus(left, right):
+    return (left.astype(F32) + right.astype(F32)).astype(BF)
+
+
+def scatter_steps(keep, send):
+    width = keep.shape[1]
+    (send,) = yield (send,)
+    came = swap(send, "c")
+
+    def part(i):
+        rows = slice(i * 128, (i + 1) * 128)
+        return plus(keep[rows], came[rows])
+
+    a_send, b_send = yield (part(1), part(3))
+    a_got = swap(a_send, "y")
+    b_got = swap(b_send, "x")
+    a_keep, b_keep = part(0), part(2)
+    a_next, b_next = yield (
+        plus(a_keep[64:], a_got[64:]),
+        plus(b_keep[64:], b_got[64:]),
+    )
+    a_last = swap(a_next, "x")
+    b_last = swap(b_next, "y")
+    a_half = plus(a_keep[:64], a_got[:64])
+    b_half = plus(b_keep[:64], b_got[:64])
+
+    def both(i):
+        rows = slice(i * 32, (i + 1) * 32)
+        return jnp.stack(
+            [
+                plus(a_half[rows], a_last[rows]).reshape(2, 16, width),
+                plus(b_half[rows], b_last[rows]).reshape(2, 16, width),
+            ],
+            1,
+        )
+
+    (low,) = yield (both(1),)
+    low_got = swap(low, "zl")
+    kept = both(0)
+    (high,) = yield (plus(kept[1], low_got[1]),)
+    total = kept[0].astype(F32) + low_got[0].astype(F32) + swap(high, "zh").astype(F32)
+    return total.reshape(32, width)
+
+
+def rotated(values):
+    lane = lax.broadcasted_iota(jnp.int32, values.shape, 1)
+    return jnp.where((lane & 63) < 32, pltpu.roll(values, 96, 1), pltpu.roll(values, 32, 1))
+
+
+def qkv_kernel(tok_ref, gain_ref, w_ref, cos_ref, sin_ref, first_ref, out_ref):
+    j = pl.program_id(0)
+
+    @pl.when(j == 0)
+    def _():
+        def chunk(i, carry):
+            rows = pl.ds(pl.multiple_of(i * 128, 128), 128)
+            normed, _ = standardize(tok_ref[rows, :].astype(F32))
+            first_ref[rows, :] = (normed * gain_ref[...]).astype(BF)
+            return carry
+
+        lax.fori_loop(0, 8, chunk, 0)
+
+    for r in range(2):
+        rows = slice(r * 512, (r + 1) * 512)
+        acc = nn(first_ref[rows, :], w_ref[...])
+
+        @pl.when(j < 4)
+        def _():
+            scale = jnp.where(j < 2, 0.125, 1.0)
+            for i in range(4):
+                part = acc[:, i * 128 : (i + 1) * 128]
+                turned = part * cos_ref[rows, :] + rotated(part) * sin_ref[rows, :]
+                out_ref[rows, i * 128 : (i + 1) * 128] = (turned * scale).astype(BF)
+
+        @pl.when(j >= 4)
+        def _():
+            out_ref[rows, :] = acc.astype(BF)
+
+
+def qkv_call(rows_in, gain, w_qkv, cosine, sine):
+    whole = lambda shape: pl.BlockSpec(shape, lambda j: (0, 0))
+    return pl.pallas_call(
+        qkv_kernel,
+        grid=(6,),
+        out_shape=[jax.ShapeDtypeStruct((1024, 1024), BF), jax.ShapeDtypeStruct((1024, 3072), BF)],
+        in_specs=[
+            whole((1024, 1024)),
+            whole((1, 1024)),
+            pl.BlockSpec((1024, 512), lambda j: (0, j)),
+            whole((1024, 128)),
+            whole((1024, 128)),
+        ],
+        out_specs=[whole((1024, 1024)), pl.BlockSpec((1024, 512), lambda j: (0, j))],
+        cost_estimate=cost(20),
+        name="norm_qkv",
+    )(rows_in, gain, w_qkv, cosine, sine)
+
+
+ROWS = 256
+
+
+def attend_kernel(q_ref, k_ref, v_ref, *refs):
+    out_ref, lse_ref = refs[-2:]
+    keys, values = k_ref[...], v_ref[...]
+
+    def chunk(i, carry):
+        rows = pl.ds(pl.multiple_of(i * ROWS, ROWS), ROWS)
+        q = q_ref[rows, :]
+        low_half = lax.broadcasted_iota(jnp.int32, (ROWS, 128), 1) < 64
+        zero = jnp.zeros_like(q)
+        outs, stats = [], []
+        for part in (jnp.where(low_half, q, zero), jnp.where(low_half, zero, q)):
+            scores = nt(part, keys)
+            peak = jnp.max(scores, -1, keepdims=True)
+            weights = jnp.exp(scores - peak)
+            total = jnp.sum(weights, -1, keepdims=True)
+            outs.append(nn(weights.astype(BF), values) / total)
+            stats.append(peak + jnp.log(total))
+        out_ref[rows, :] = jnp.where(low_half, outs[0], outs[1]).astype(BF)
+        lse_ref[rows, :] = jnp.where(low_half, stats[0], stats[1])
+        return carry
+
+    lax.fori_loop(0, 1024 // ROWS, chunk, 0)
+
+
+def head_spec(offset):
+    return pl.BlockSpec((1024, 128), lambda j: (0, offset + j))
+
+
+def attend_call(qkv, start, count, carry):
+    operands, in_specs, aliases = [qkv] * 3, [head_spec(i + start) for i in (0, 8, 16)], {}
+    if carry is not None:
+        operands += list(carry)
+        in_specs += [ANY, ANY]
+        aliases = {3: 0, 4: 1}
+    return pl.pallas_call(
+        attend_kernel,
+        grid=(count,),
+        out_shape=[jax.ShapeDtypeStruct((1024, 1024), BF), jax.ShapeDtypeStruct((1024, 1024), F32)],
+        in_specs=in_specs,
+        out_specs=[head_spec(start)] * 2,
+        input_output_aliases=aliases,
+        cost_estimate=cost(5 * count),
+        name="attend",
+    )(*operands)
+
+
+def attend_back_kernel(
+    q_ref, k_ref, v_ref, att_ref, lse_ref, datt_ref, cos_ref, sin_ref, *refs
+):
+    out_ref, qt, dt, dkt, dvt = refs[-5:]
+    keys, values = k_ref[...], v_ref[...]
+    lane = lax.broadcasted_iota(jnp.int32, (1024, 128), 1) < 64
+    nothing = jnp.zeros_like(keys)
+    key_parts = (jnp.where(lane, keys, nothing), jnp.where(lane, nothing, keys))
+    for i in range(1024 // ROWS):
+        rows = slice(i * ROWS, (i + 1) * ROWS)
+        qt[i] = q_ref[rows, :].astype(F32).T.astype(BF)
+        dt[i] = datt_ref[rows, :].astype(F32).T.astype(BF)
+    dkt[...] = jnp.zeros_like(dkt)
+    dvt[...] = jnp.zeros_like(dvt)
+
+    def chunk(i, carry):
+        rows = pl.ds(pl.multiple_of(i * ROWS, ROWS), ROWS)
+        q, datt = q_ref[rows, :], datt_ref[rows, :]
+        low_half = lax.broadcasted_iota(jnp.int32, (ROWS, 128), 1) < 64
+        zero = jnp.zeros_like(q)
+        mixed = datt.astype(F32) * att_ref[rows, :].astype(F32)
+        grad_q = jnp.zeros((ROWS, 128), F32)
+        for h in range(2):
+            def pick(t, z):
+                return jnp.where(low_half, t, z) if h == 0 else jnp.where(low_half, z, t)
+
+            delta = jnp.sum(pick(mixed, jnp.zeros_like(mixed)), -1, keepdims=True)
+            lse = lse_ref[rows, h * 64 : h * 64 + 1]
+            probs = jnp.exp(nt(pick(q, zero), keys) - lse)
+            grad_probs = nt(pick(datt, zero), values)
+            grad_scores = (probs * (grad_probs - delta)).astype(BF)
+            grad_q += nn(grad_scores, key_parts[h])
+            side = slice(h * 64, (h + 1) * 64)
+            dkt[side, :] += nn(qt[i, side, :], grad_scores)
+            dvt[side, :] += nn(dt[i, side, :], probs.astype(BF))
+        grad_q = grad_q * 0.125
+        grad_q = grad_q * cos_ref[rows, :] - rotated(grad_q) * sin_ref[rows, :]
+        out_ref[0, rows, :] = grad_q.astype(BF)
+        return carry
+
+    lax.fori_loop(0, 1024 // ROWS, chunk, 0)
+    grad_k = dkt[...].T
+    grad_k = grad_k * cos_ref[...] - rotated(grad_k) * sin_ref[...]
+    out_ref[1] = grad_k.astype(BF)
+    out_ref[2] = dvt[...].T.astype(BF)
+
+
+def attend_back_call(qkv, attended, lse, datt, cosine, sine, start, count, carry):
+    table = pl.BlockSpec((1024, 128), lambda j: (0, 0))
+    operands = [qkv, qkv, qkv, attended, lse, datt, cosine, sine]
+    in_specs = [head_spec(i + start) for i in (0, 8, 16, 0, 0, 0)] + [table] * 2
+    aliases = {}
+    if carry is not None:
+        operands.append(carry)
+        in_specs.append(ANY)
+        aliases = {8: 0}
+    return pl.pallas_call(
+        attend_back_kernel,
+        grid=(count,),
+        out_shape=jax.ShapeDtypeStruct((3, 1024, 1024), BF),
+        in_specs=in_specs,
+        out_specs=pl.BlockSpec((3, 1024, 128), lambda j: (0, 0, start + j)),
+        scratch_shapes=[
+            pltpu.VMEM((1024 // ROWS, 128, ROWS), BF),
+            pltpu.VMEM((1024 // ROWS, 128, ROWS), BF),
+            pltpu.VMEM((128, 1024), F32),
+            pltpu.VMEM((128, 1024), F32),
+        ],
+        input_output_aliases=aliases,
+        cost_estimate=cost(7.5 * count),
+        name="attend_back",
+    )(*operands)
+
+
+def feed_kernel(second_ref, grad_ref, gate_ref, up_ref, down_ref, hid_ref, dgate_ref, dup_ref):
+    def chunk(i, carry):
+        rows = pl.ds(pl.multiple_of(i * 256, 256), 256)
+        second = second_ref[rows, :]
+        gate = nn(second, gate_ref[...])
+        up = nn(second, up_ref[...])
+        grad = nn(grad_ref[rows, :], down_ref[...])
+        below = 0.5 + 0.5 * lax.erf(gate * math.sqrt(0.5))
+        active = gate * below
+        slope = below + gate * jnp.exp(-0.5 * gate * gate) * (1.0 / math.sqrt(2.0 * math.pi))
+        hid_ref[rows, :] = (active * up).astype(BF)
+        dgate_ref[rows, :] = (grad * up * slope).astype(BF)
+        dup_ref[rows, :] = (grad * active).astype(BF)
+        return carry
+
+    lax.fori_loop(0, 4, chunk, 0)
+
+
+def feed_call(second, grad_low, w_gate, w_up, w_down_t):
+    width, block = w_gate.shape[1], 896
+    rows = pl.BlockSpec((1024, 1024), lambda j: (0, 0))
+    cols = pl.BlockSpec((1024, block), lambda j: (0, j))
+    return pl.pallas_call(
+        feed_kernel,
+        grid=(width // block,),
+        out_shape=[jax.ShapeDtypeStruct((1024, width), BF)] * 3,
+        in_specs=[rows, rows, cols, cols, cols],
+        out_specs=[cols] * 3,
+        cost_estimate=cost(30),
+        name="feed",
+    )(second, grad_low, w_gate, w_up, w_down_t)
+
+
+def whole_rows(local, place):
+    own = lax.dynamic_index_in_dim(local, place, 0, keepdims=False)
+    got = swap(lax.dynamic_index_in_dim(local, 1 - place, 0, keepdims=False), "x")
+    return jnp.where(
+        place == 0, jnp.concatenate([own, got], 0), jnp.concatenate([got, own], 0)
+    )
+
+
+def half_rows(whole, place):
+    half = whole.shape[0] // 2
+    own = lax.dynamic_slice_in_dim(whole, place * half, half, 0)
+    got = swap(lax.dynamic_slice_in_dim(whole, (1 - place) * half, half, 0), "x")
+    return jnp.where(place == 0, jnp.stack([own, got]), jnp.stack([got, own]))
+
+
+def paired_body(tokens, cotangent, w_qkv, w_out, w_gate, w_up, w_down, gain_one, gain_two):
+    features = w_gate.shape[1]
+    padded = -(-features // 896) * 896
+    coords = jnp.stack([lax.axis_index(name) for name in BITS]).astype(jnp.int32)
+    place = coords[4]
+    barrier = lax.optimization_barrier
+
+    def pad(array):
+        return jnp.pad(array, ((0, 0), (0, padded - features)))
+
+    gains = jnp.pad(jnp.stack([gain_one, gain_two], 1), ((0, 0), (0, 126)))
+    shard_two = jnp.concatenate([pad(w_gate), pad(w_up), w_out], 1)
+    shard_three = pad(w_down.T)
+    cosine, sine = rotary_tables(1024, 0, HEAD_DIM)
+    sign = jnp.where(jnp.arange(HEAD_DIM) < HEAD_DIM // 2, -1.0, 1.0)
+    cosine = jnp.concatenate([cosine, cosine], 1)
+    sine = jnp.concatenate([sine * sign, sine * sign], 1)
+
+    one = Chain(gather_steps(jnp.concatenate([w_qkv, gains], 1)))
+    one.go()
+    rows_in = whole_rows(tokens, place)
+    one.go()
+    shard_two, shard_three, cotangent = one.go(shard_two, shard_three, cotangent)
+    two = Chain(gather_steps(shard_two))
+    two.go()
+    one.go()
+    two.go()
+    one.go()
+    full_qkv = assemble(one.value, coords, 3072, 1024, 0)
+    gain_cols = assemble(one.value, coords, 128, 128, 24)
+    shard_three, cotangent = two.go(shard_three, cotangent)
+    three = Chain(gather_steps(shard_three))
+    three.go()
+    gain_rows = gain_cols[:, :2].astype(F32).T
+    full_one, full_two = gain_rows[0:1], gain_rows[1:2]
+
+    first, qkv = qkv_call(rows_in, full_one, full_qkv, cosine, sine)
+    qkv = two.go(qkv)
+    qkv = three.go(qkv)
+    halves = attend_call(qkv, 0, 4, None)
+    halves = three.go(*halves)
+    halves, cotangent = barrier((halves, cotangent))
+    grad_low = whole_rows(cotangent, place)
+    attended, lse = attend_call(qkv, 4, 4, halves)
+    attended = two.go(attended)
+    attended = three.go(attended)
+    full_out = assemble(two.value, coords, 1024, 256, 2 * padded // 256)
+    full_gate = assemble(two.value, coords, padded, 896, 0)
+    full_up = assemble(two.value, coords, padded, 896, padded // 896)
+
+    inputs_f = rows_in.astype(F32)
+    residual = inputs_f + nn(attended, full_out)
+    normed_two, inverse_two = standardize(residual)
+    second = (normed_two * full_two).astype(BF)
+    second = three.go(second)
+    full_down = assemble(three.value, coords, padded, 896, 0)
+    hidden, d_gate, d_up = feed_call(second, grad_low, full_gate, full_up, full_down)
+
+    block = 896
+    col_spec = pl.BlockSpec((1024, block), lambda j: (0, j))
+    per = padded // block
+
+    def grad_of(left, right, start, total, carry):
+        return grad_call(coords, left, right, col_spec, padded, block, total, start, carry)
+
+    down = Chain(scatter_steps(*grad_of(grad_low, hidden, 0, padded, None)))
+    d_gate = down.go(d_gate)
+    sums = grad_of(second, d_gate, 0, 2 * padded, None)
+    sums, d_up = down.go(sums, d_up)
+    sums = grad_of(second, d_up, per, 2 * padded, sums)
+    feed = Chain(scatter_steps(*sums))
+    d_gate = feed.go(d_gate)
+    d_gate = down.go(d_gate)
+    grad_second = nt(d_gate, full_gate)
+    grad_second, d_up = feed.go(grad_second, d_up)
+    grad_second, d_up = down.go(grad_second, d_up)
+    grad_second = grad_second + nt(d_up, full_up)
+    grad_resid, part_two = norm_back(grad_second, normed_two, inverse_two, full_two)
+    grad_resid = grad_resid + grad_low.astype(F32)
+    grad_proj = grad_resid.astype(BF)
+    grad_proj = down.go(grad_proj)
+    datt = nt(grad_proj, full_out).astype(BF)
+    out_spec = pl.BlockSpec((1024, 512), lambda j: (0, j))
+    out = Chain(
+        scatter_steps(*grad_call(coords, attended, grad_proj, out_spec, 1024, 512, 1024, 0, None))
+    )
+    datt = out.go(datt)
+    fused = attend_back_call(qkv, attended, lse, datt, cosine, sine, 0, 2, None)
+    fused = feed.go(fused)
+    fused = out.go(fused)
+    fused = attend_back_call(qkv, attended, lse, datt, cosine, sine, 2, 2, fused)
+    fused = feed.go(fused)
+    fused = out.go(fused)
+    outcome = (residual + nt(hidden, full_down)).astype(BF)
+    fused, outcome = barrier((fused, outcome))
+    result = half_rows(outcome, place)
+    fused = attend_back_call(qkv, attended, lse, datt, cosine, sine, 4, 2, fused)
+    fused = feed.go(fused)
+    fused = out.go(fused)
+    fused = attend_back_call(qkv, attended, lse, datt, cosine, sine, 6, 2, fused)
+    fused = out.go(fused)
+
+    qkv_spec = pl.BlockSpec((1, 1024, 1024), lambda j: (j, 0, 0))
+    last = Chain(
+        scatter_steps(*grad_call(coords, first, fused, qkv_spec, 3072, 1024, 3072, 0, None))
+    )
+    fused = last.go(fused)
+    grad_first = nt(fused[0], full_qkv[:, :1024])
+    grad_first, fused = last.go(grad_first, fused)
+    grad_first = grad_first + nt(fused[1], full_qkv[:, 1024:2048])
+    grad_first = grad_first + nt(fused[2], full_qkv[:, 2048:])
+    grad_first = last.go(grad_first)
+    normed_one, inverse_one = standardize(inputs_f)
+    grad_in, part_one = norm_back(grad_first, normed_one, inverse_one, full_one)
+    input_grad = half_rows((grad_in + grad_resid).astype(BF), place)
+    parts = jnp.stack([part_one, part_two])
+    for axis in BITS:
+        parts = parts + swap(parts, axis)
+    index = ((((coords[0] * 2 + coords[1]) * 2 + coords[2]) * 2 + coords[3]) * 2 + coords[4]) * 32
+    parts = lax.dynamic_slice_in_dim(parts, index, 32, 1)
+    last.go()
+    last.go()
+    return (
+        result,
+        input_grad,
+        last.value,
+        out.value,
+        feed.value[:, :features],
+        feed.value[:, padded : padded + features],
+        down.value[:, :features].T,
+        parts[0],
+        parts[1],
+    )
+
+
 def solution(mesh):
-    in_specs = (
-        P("dp", "ctx", None),
-        P("dp", "ctx", None),
-        P(("dp", "ctx"), None),
-        P(("dp", "ctx"), None),
-        P(("dp", "ctx"), None),
-        P(("dp", "ctx"), None),
-        P(None, ("dp", "ctx")),
-        P(("dp", "ctx")),
-        P(("dp", "ctx")),
-    )
-    out_specs = (
-        P("dp", "ctx", None),
-        P("dp", "ctx", None),
-        P(("dp", "ctx"), None),
-        P(("dp", "ctx"), None),
-        P(("dp", "ctx"), None),
-        P(("dp", "ctx"), None),
-        P(None, ("dp", "ctx")),
-        P(("dp", "ctx")),
-        P(("dp", "ctx")),
-    )
-    return jax.shard_map(body, mesh=mesh, in_specs=in_specs, out_specs=out_specs, check_vma=False)
+    groups, pair = mesh.shape["dp"], mesh.shape["ctx"]
+    if (groups, pair) == (16, 2):
+        mesh = jax.sharding.Mesh(mesh.devices.reshape(2, 2, 2, 2, 2), BITS)
+        outer, inner, run = BITS[:4], "x", paired_body
+    else:
+        outer, inner, run = "dp", "ctx", body
+    every = BITS if run is paired_body else ("dp", "ctx")
+    whole, rows, cols, line = P(outer, inner, None), P(every, None), P(None, every), P(every)
+    in_specs = (whole, whole, rows, rows, rows, rows, cols, line, line)
+    out_specs = (whole, whole, rows, rows, rows, rows, cols, line, line)
+    return jax.shard_map(run, mesh=mesh, in_specs=in_specs, out_specs=out_specs, check_vma=False)

time: 1550 us -> 627 us (0.40)
  waiting for transfers between devices: 829 us -> 184 us
  matrix products: 351 us -> 53.7 us
  Pallas kernels: 0 us -> 243 us
  local copies, waits for them, and re-layouts: 136 us -> 13.8 us
  blocking collectives: 82.8 us -> 0 us
  starting transfers between devices: 0.77 us -> 64.3 us
  other arithmetic: 123 us -> 61.7 us
    reduce_scatter x6 -> x0, waiting for transfers between devices: 446 us -> none  [the longest x1 160 us: body(): lax.psum_scatter(local_grads[0], ('dp', 'ctx'), scatter_dimension=0, tile...]
    dot_general x21 -> x8, matrix products: 351 us -> 53.7 us  [the longest x7 49.1 us: nt(): lax.dot_general(left, right, (((1,), (1,)), ((), ())), preferred_element_...]
    pallas_call x0 -> x19, Pallas kernels: none -> 243 us  [the longest x4 67.3 us: attend_back_call(): pl.pallas_call(attend_back_kernel, grid=(count,), out_shape=jax.ShapeDtyp...]
    all_gather x7 -> x0, waiting for transfers between devices: 230 us -> none  [the longest x1 58.7 us: body(): lax.all_gather(shards[2], ('dp', 'ctx'), axis=0, tiled=True)]
    ppermute x0 -> x67, waiting for transfers between devices: none -> 184 us  [swap(): return lax.ppermute(values, axis, [(0, 1), (1, 0)])]
    unnamed x15 -> x0, waiting for transfers between devices: 153 us -> none
    unnamed x2 -> x0, blocking collectives: 82.8 us -> none
    ppermute x0 -> x67, starting transfers between devices: none -> 64.3 us  [swap(): return lax.ppermute(values, axis, [(0, 1), (1, 0)])]
  transfers between devices with their start and end apart: 14 -> 67, of which waited for: 11 -> 27; matrix products, arithmetic and copies ran while one was open for 27% -> 17% of each run, Pallas kernels for 0% -> 28%
where the time goes in v1:
time: 627 us; the launch traced here: 622 us
  Pallas kernels  243 us (39%)
  waiting for transfers between devices  184 us (29%)
  starting transfers between devices  64.3 us (10%)
  other arithmetic  61.7 us (10%)
  matrix products  53.7 us (9%)
  local copies, waits for them, and re-layouts  13.8 us (2%)
    ppermute x67, waiting for transfers between devices, swap(): return lax.ppermute(values, axis, [(0, 1), (1, 0)])  184 us
    pallas_call x4, Pallas kernels, attend_back_call(): pl.pallas_call(attend_back_kernel, grid=(count,), out_shape=jax.ShapeDtyp...  67.3 us
    ppermute x67, starting transfers between devices, swap(): return lax.ppermute(values, axis, [(0, 1), (1, 0)])  64.3 us
    pallas_call x5, Pallas kernels, grad_call(): pl.pallas_call(grad_kernel, grid=(steps,), out_shape=[jax.ShapeDtypeStruc...  54.3 us
    dot_general x7, matrix products, nt(): lax.dot_general(left, right, (((1,), (1,)), ((), ())), preferred_element_...  49.1 us
    pallas_call x2, Pallas kernels, attend_call(): pl.pallas_call(attend_kernel, grid=(count,), out_shape=[jax.ShapeDtypeStr...  41.1 us
    pallas_call x6, Pallas kernels, assemble(): pl.pallas_call(assemble_kernel, grid=(width // block,), out_shape=jax.Sha...  30.9 us
    pallas_call x1, Pallas kernels, feed_call(): pl.pallas_call(feed_kernel, grid=(width // block,), out_shape=[jax.ShapeD...  29.4 us
  transfers between devices with their start and end apart: 67, of which 27 were waited for; matrix products, arithmetic and copies ran while one was open for 17% of the time, Pallas kernels for 28%

profile of v1, /device:TPU:0, one launch (start us, length us, event | category | flops | bytes accessed | tf_op | source)
XLA Modules:
  0.0 621.8 jit_solution(12956427084028960861)
XLA Ops:
  17.6 9.2 %collective-permute-done.2 = bf16[2,2,16,3200]{3,2,0,1:T(8,128)(2,1)S(1)} collective-permute-done((bf16[2,2,16,3200]{3,2,0,1:T(8,128)(2,1)S(1)}, bf16[2,2,16,3200]{3,2,0,1:T(8,128)(2,1)S(1)}, u32[]{:S(2)}, u32[]{:S(2)}) %collective-permute-start.2) | collective-permute-done | bytes 409632 | tf_op jit(solution)/shard_map/ppermute | solution.py:234
  33.2 8.8 %collective-permute-done.5 = bf16[4,16,3200]{2,1,0:T(8,128)(2,1)S(1)} collective-permute-done((bf16[4,16,3200]{2,1,0:T(8,128)(2,1)S(1)}, bf16[4,16,3200]{2,1,0:T(8,128)(2,1)S(1)}, u32[]{:S(2)}, u32[]{:S(2)}) %collective-permute-start.5) | collective-permute-done | bytes 409632 | tf_op jit(solution)/shard_map/ppermute | solution.py:234
  50.4 18.3 %collective-permute-done.12 = bf16[2,2,16,6400]{3,2,0,1:T(8,128)(2,1)S(1)} collective-permute-done((bf16[2,2,16,6400]{3,2,0,1:T(8,128)(2,1)S(1)}, bf16[2,2,16,6400]{3,2,0,1:T(8,128)(2,1)S(1)}, u32[]{:S(2)}, u32[]{:S(2)}) %collective-permute-start.12) | collective-permute-done | bytes 819232 | tf_op jit(solution)/shard_map/ppermute | solution.py:234
  70.5 16.7 %collective-permute-done.4.refs_1_ = bf16[8,16,3200]{2,1,0:T(8,128)(2,1)S(1)} collective-permute-done((bf16[8,16,3200]{2,1,0:T(8,128)(2,1)S(1)}, bf16[8,16,3200]{2,1,0:T(8,128)(2,1)S(1)}, u32[]{:S(2)}, u32[]{:S(2)}) %collective-permute-start.4) | collective-permute-done | bytes 819232 | tf_op jit(solution)/shard_map/ppermute | solution.py:234
  114.5 19.8 %norm_qkv.1 = (bf16[1024,1024]{1,0:T(8,128)(2,1)}, bf16[1024,3072]{1,0:T(8,128)(2,1)}) custom-call(bf16[1024,1024]{1,0:T(8,128)(2,1)} %get-tuple-element.224.tok_ref, f32[1,1024]{1,0:T(1,128)} %get-tuple-element.298.gain_ref, bf16[1024,3072]{1,0:T(8,128)(2,1)} %assemble.7.w_ref, f32[1024,128]{1,0:T(8,128)} %get-tuple-element.308.cos_ref, ...), custom_call_target="tpu_custom_call" | custom-call | flops 14000000000 | bytes 20000000 | tf_op jit(solution)/shard_map/norm_qkv/pallas_call | solution.py:443
  142.3 20.5 %attend.2 = (bf16[1024,1024]{1,0:T(8,128)(2,1)}, f32[1024,1024]{1,0:T(8,128)}) custom-call(bf16[1024,3072]{1,0:T(8,128)(2,1)} %get-tuple-element.123.q_ref.k_ref.v_ref, bf16[1024,3072]{1,0:T(8,128)(2,1)} %get-tuple-element.123.q_ref.k_ref.v_ref, bf16[1024,3072]{1,0:T(8,128)(2,1)} %get-tuple-element.123.q_ref.k_ref.v_ref), custom_call_target="tpu_custom_call" | custom-call | flops 14000000000 | bytes 20000000 | tf_op jit(solution)/shard_map/attend/pallas_call | solution.py:497
  163.7 20.7 %attend.3 = (bf16[1024,1024]{1,0:T(8,128)(2,1)}, f32[1024,1024]{1,0:T(8,128)}) custom-call(bf16[1024,3072]{1,0:T(8,128)(2,1)} %get-tuple-element.123.q_ref.k_ref.v_ref, bf16[1024,3072]{1,0:T(8,128)(2,1)} %get-tuple-element.123.q_ref.k_ref.v_ref, ...), custom_call_target="tpu_custom_call", output_to_operand_aliasing={{0}: (3, {}), {1}: (4, {})} | custom-call | flops 14000000000 | bytes 20000000 | tf_op jit(solution)/shard_map/attend/pallas_call | solution.py:497
  187.2 8.6 %collective-permute-done.19 = bf16[4,16,2688]{2,1,0:T(8,128)(2,1)S(1)} collective-permute-done((bf16[4,16,2688]{2,1,0:T(8,128)(2,1)}, bf16[4,16,2688]{2,1,0:T(8,128)(2,1)S(1)}, u32[]{:S(2)}, u32[]{:S(2)}) %collective-permute-start.19) | collective-permute-done | bytes 344096 | tf_op jit(solution)/shard_map/ppermute | solution.py:234
  222.1 21.3 %collective-permute-done.26.refs_3_ = bf16[8,16,2688]{2,1,0:T(8,128)(2,1)} collective-permute-done((bf16[8,16,2688]{2,1,0:T(8,128)(2,1)}, bf16[8,16,2688]{2,1,0:T(8,128)(2,1)}, u32[]{:S(2)}, u32[]{:S(2)}) %collective-permute-start.26) | collective-permute-done | bytes 688160 | tf_op jit(solution)/shard_map/ppermute | solution.py:234
  267.0 29.4 %feed.1 = (bf16[1024,2688]{1,0:T(8,128)(2,1)}, bf16[1024,2688]{1,0:T(8,128)(2,1)}, bf16[1024,2688]{1,0:T(8,128)(2,1)}) custom-call(bf16[1024,1024]{1,0:T(8,128)(2,1)} %multiply_convert_fusion.second_ref.x_ref, bf16[1024,1024]{1,0:T(8,128)(2,1)} %maximum_select_fusion.1.grad_ref.x_ref, bf16[1024,2688]{1,0:T(8,128)(2,1)} %assemble.9.gate_ref, ...), custom_call_target="tpu_custom_call" | custom-call | flops 20999999488 | bytes 30000000 | tf_op jit(solution)/shard_map/feed/pallas_call | solution.py:605
  296.4 11.7 %weight_grad.5 = (bf16[512,2688]{1,0:T(8,128)(2,1)}, bf16[512,2688]{1,0:T(8,128)(2,1)}) custom-call(s32[5]{0:T(128)} %stack.111.coords, bf16[1024,1024]{1,0:T(8,128)(2,1)} %maximum_select_fusion.1.grad_ref.x_ref, bf16[1024,2688]{1,0:T(8,128)(2,1)} %get-tuple-element.153.y_ref), custom_call_target="tpu_custom_call" | custom-call | flops 8180869632 | bytes 11686956 | tf_op jit(solution)/shard_map/weight_grad/pallas_call | solution.py:349
  309.4 11.9 %weight_grad.6 = (bf16[512,5376]{1,0:T(8,128)(2,1)}, bf16[512,5376]{1,0:T(8,128)(2,1)}) custom-call(s32[5]{0:T(128)} %stack.111.coords, bf16[1024,1024]{1,0:T(8,128)(2,1)} %multiply_convert_fusion.second_ref.x_ref, bf16[1024,2688]{1,0:T(8,128)(2,1)} %get-tuple-element.168.y_ref), custom_call_target="tpu_custom_call" | custom-call | flops 8180869632 | bytes 11686956 | tf_op jit(solution)/shard_map/weight_grad/pallas_call | solution.py:349
  324.8 11.8 %weight_grad.7 = (bf16[512,5376]{1,0:T(8,128)(2,1)}, bf16[512,5376]{1,0:T(8,128)(2,1)}) custom-call(s32[5]{0:T(128)} %stack.111.coords, bf16[1024,1024]{1,0:T(8,128)(2,1)} %multiply_convert_fusion.second_ref.x_ref, bf16[1024,2688]{1,0:T(8,128)(2,1)} %get-tuple-element.176.y_ref, ...), custom_call_target="tpu_custom_call", output_to_operand_aliasing={{0}: (3, {}), {1}: (4, {})} | custom-call | flops 8180869632 | bytes 11686956 | tf_op jit(solution)/shard_map/weight_grad/pallas_call | solution.py:349
  338.1 12.0 %add_convert_fusion = bf16[1024,1024]{1,0:T(8,128)(2,1)} fusion(f32[1024,1024]{1,0:T(8,128)} %copy-done, bf16[1024,2688]{1,0:T(8,128)(2,1)} %get-tuple-element.153.y_ref, bf16[1024,2688]{1,0:T(8,128)(2,1)} %assemble.11.down_ref), kind=kOutput, calls=%fused_computation.17 | convolution fusion | flops 5639241728 | bytes 17301504 | tf_op jit(solution)/shard_map/dot_general | solution.py:238
  354.7 13.0 %collective-permute-done.34 = bf16[128,2688]{1,0:T(8,128)(2,1)S(1)} collective-permute-done((bf16[128,2688]{1,0:T(8,128)(2,1)S(1)}, bf16[128,2688]{1,0:T(8,128)(2,1)S(1)}, u32[]{:S(2)}, u32[]{:S(2)}) %collective-permute-start.34) | collective-permute-done | bytes 688160 | tf_op jit(solution)/shard_map/ppermute | solution.py:234
  368.5 9.8 %fusion.68 = f32[1024,1024]{1,0:T(8,128)} fusion(bf16[1024,2688]{1,0:T(8,128)(2,1)} %get-tuple-element.168.y_ref, bf16[1024,2688]{1,0:T(8,128)(2,1)S(1)} %bitcast.190), kind=kOutput, calls=%fused_computation.228 | convolution fusion | flops 5637144576 | bytes 15204352 | tf_op jit(solution)/shard_map/dot_general | solution.py:238
  390.6 9.9 %multiply_reduce_fusion = (f32[1024]{0:T(1024)S(1)}, f32[1024]{0:T(1024)S(1)}, f32[1024]{0:T(1024)S(1)}, f32[1024,1024]{1,0:T(8,128)S(1)}) fusion(f32[1024,1024]{1,0:T(8,128)S(1)} %copy-done.1, f32[1024]{0:T(1024)S(1)} %add_rsqrt_fusion.1, f32[1024]{0:T(1024)S(1)} %broadcast_multiply_fusion.5, f32[1024]{0:T(1024)S(1)} %bitcast.244, ...), kind=kOutput, calls=%fused_computation.15 | convolution fusion | flops 5646578688 | bytes 23617536 | tf_op jit(solution)/shard_map/dot_general | solution.py:238
  423.2 16.8 %attend_back.4.refs_0_ = bf16[3,1024,1024]{2,1,0:T(8,128)(2,1)} custom-call(bf16[1024,3072]{1,0:T(8,128)(2,1)} %get-tuple-element.123.q_ref.k_ref.v_ref, bf16[1024,3072]{1,0:T(8,128)(2,1)} %get-tuple-element.123.q_ref.k_ref.v_ref, bf16[1024,3072]{1,0:T(8,128)(2,1)} %get-tuple-element.123.q_ref.k_ref.v_ref, ...), custom_call_target="tpu_custom_call" | custom-call | flops 10499999744 | bytes 15000000 | tf_op jit(solution)/shard_map/attend_back/pallas_call | solution.py:565
  453.4 16.8 %attend_back.5.refs_0_ = bf16[3,1024,1024]{2,1,0:T(8,128)(2,1)} custom-call(bf16[1024,3072]{1,0:T(8,128)(2,1)} %get-tuple-element.123.q_ref.k_ref.v_ref, bf16[1024,3072]{1,0:T(8,128)(2,1)} %get-tuple-element.123.q_ref.k_ref.v_ref, bf16[1024,3072]{1,0:T(8,128)(2,1)} %get-tuple-element.123.q_ref.k_ref.v_ref, ...), custom_call_target="tpu_custom_call", output_to_operand_aliasing={{}: (8, {})} | custom-call | flops 10499999744 | bytes 15000000 | tf_op jit(solution)/shard_map/attend_back/pallas_call | solution.py:565
  478.6 16.8 %attend_back.6.refs_0_ = bf16[3,1024,1024]{2,1,0:T(8,128)(2,1)} custom-call(bf16[1024,3072]{1,0:T(8,128)(2,1)} %get-tuple-element.123.q_ref.k_ref.v_ref, bf16[1024,3072]{1,0:T(8,128)(2,1)} %get-tuple-element.123.q_ref.k_ref.v_ref, bf16[1024,3072]{1,0:T(8,128)(2,1)} %get-tuple-element.123.q_ref.k_ref.v_ref, ...), custom_call_target="tpu_custom_call", output_to_operand_aliasing={{}: (8, {})} | custom-call | flops 10499999744 | bytes 15000000 | tf_op jit(solution)/shard_map/attend_back/pallas_call | solution.py:565
  498.2 16.8 %attend_back.7.y_ref = bf16[3,1024,1024]{2,1,0:T(8,128)(2,1)} custom-call(bf16[1024,3072]{1,0:T(8,128)(2,1)} %get-tuple-element.123.q_ref.k_ref.v_ref, bf16[1024,3072]{1,0:T(8,128)(2,1)} %get-tuple-element.123.q_ref.k_ref.v_ref, bf16[1024,3072]{1,0:T(8,128)(2,1)} %get-tuple-element.123.q_ref.k_ref.v_ref, ...), custom_call_target="tpu_custom_call", output_to_operand_aliasing={{}: (8, {})} | custom-call | flops 10499999744 | bytes 15000000 | tf_op jit(solution)/shard_map/attend_back/pallas_call | solution.py:565
  515.1 12.3 %weight_grad.9 = (bf16[512,3072]{1,0:T(8,128)(2,1)}, bf16[512,3072]{1,0:T(8,128)(2,1)}) custom-call(s32[5]{0:T(128)} %stack.111.coords, bf16[1024,1024]{1,0:T(8,128)(2,1)} %get-tuple-element.202.x_ref, bf16[3,1024,1024]{2,1,0:T(8,128)(2,1)} %attend_back.7.y_ref), custom_call_target="tpu_custom_call" | custom-call | flops 9349565440 | bytes 13356521 | tf_op jit(solution)/shard_map/weight_grad/pallas_call | solution.py:349
  539.9 13.4 %collective-permute-done.59 = bf16[2,16,1024]{2,1,0:T(8,128)(2,1)S(1)} collective-permute-done((bf16[2,16,1024]{2,1,0:T(8,128)(2,1)S(1)}, bf16[2,16,1024]{2,1,0:T(8,128)(2,1)S(1)}, u32[]{:S(2)}, u32[]{:S(2)}) %collective-permute-start.59) | collective-permute-done | bytes 65568 | tf_op jit(solution)/shard_map/ppermute | solution.py:234
  566.4 9.3 %collective-permute-done.52 = bf16[128,3072]{1,0:T(8,128)(2,1)S(1)} collective-permute-done((bf16[128,3072]{1,0:T(8,128)(2,1)S(1)}, bf16[128,3072]{1,0:T(8,128)(2,1)S(1)}, u32[]{:S(2)}, u32[]{:S(2)}) %collective-permute-start.52) | collective-permute-done | bytes 786464 | tf_op jit(solution)/shard_map/ppermute | solution.py:234
  (336 shorter events, 264.3 us)
Async XLA Ops:
  9.3 78.0 %collective-permute-start = (bf16[512,1024]{1,0:T(8,128)(2,1)}, bf16[512,1024]{1,0:T(8,128)(2,1)}, u32[]{:S(2)}, u32[]{:S(2)}) collective-permute-start(bf16[512,1024]{1,0:T(8,128)(2,1)} %get-tuple-element.253), channel_id=1, source_target_pairs={{0,1},{1,0},{2,3},{3,2},{4,5},{5,4},{6,7},{7,6},{8,9},{9,8},{10,11... | collective-permute-start | bytes 3145736 | tf_op jit(solution)/shard_map/ppermute | solution.py:234
  26.9 23.3 %collective-permute-start.3 = (bf16[4,16,3200]{2,1,0:T(8,128)(2,1)S(1)}, bf16[4,16,3200]{2,1,0:T(8,128)(2,1)S(1)}, u32[]{:S(2)}, u32[]{:S(2)}) collective-permute-start(bf16[4,16,3200]{2,1,0:T(8,128)(2,1)S(1)} %get-tuple-element.113), channel_id=1, source_target_pairs={{0,1},{1,0},{2,3},{3,2},{4,5},{5,4},{6,7},{7,6},{8,9},{9,8},{10,11... | collective-permute-start | bytes 1228808 | tf_op jit(solution)/shard_map/ppermute | solution.py:234
  42.1 59.0 %collective-permute-start.9 = (bf16[8,16,3200]{2,1,0:T(8,128)(2,1)S(1)}, bf16[8,16,3200]{2,1,0:T(8,128)(2,1)S(1)}, u32[]{:S(2)}, u32[]{:S(2)}) collective-permute-start(bf16[8,16,3200]{2,1,0:T(8,128)(2,1)S(1)} %constant_dynamic-update-slice_fusion.2.refs_2_), channel_id=1, source_target_pairs={{0,2},{2,0},{1,3},{3,1},{4,6},{6,4},{5,7},{7,5},{8,10},{10,8},{9,1... | collective-permute-start | bytes 2457608 | tf_op jit(solution)/shard_map/ppermute | solution.py:234
  42.2 28.3 %collective-permute-start.6 = (bf16[8,16,3200]{2,1,0:T(8,128)(2,1)S(1)}, bf16[8,16,3200]{2,1,0:T(8,128)(2,1)S(1)}, u32[]{:S(2)}, u32[]{:S(2)}) collective-permute-start(bf16[8,16,3200]{2,1,0:T(8,128)(2,1)S(1)} %constant_dynamic-update-slice_fusion.2.refs_2_), channel_id=1, source_target_pairs={{0,1},{1,0},{2,3},{3,2},{4,5},{5,4},{6,7},{7,6},{8,9},{9,8},{10,11... | collective-permute-start | bytes 2457608 | tf_op jit(solution)/shard_map/ppermute | solution.py:234
  50.3 52.4 %collective-permute-start.7 = (bf16[8,16,3200]{2,1,0:T(8,128)(2,1)S(1)}, bf16[8,16,3200]{2,1,0:T(8,128)(2,1)S(1)}, u32[]{:S(2)}, u32[]{:S(2)}) collective-permute-start(bf16[8,16,3200]{2,1,0:T(8,128)(2,1)S(1)} %constant_dynamic-update-slice_fusion.refs_0_), channel_id=1, source_target_pairs={{0,2},{2,0},{1,3},{3,1},{4,6},{6,4},{5,7},{7,5},{8,10},{10,8},{9,1... | collective-permute-start | bytes 2457608 | tf_op jit(solution)/shard_map/ppermute | solution.py:234
  70.5 32.3 %collective-permute-start.10 = (bf16[8,16,3200]{2,1,0:T(8,128)(2,1)S(1)}, bf16[8,16,3200]{2,1,0:T(8,128)(2,1)S(1)}, u32[]{:S(2)}, u32[]{:S(2)}) collective-permute-start(bf16[8,16,3200]{2,1,0:T(8,128)(2,1)S(1)} %collective-permute-done.6.refs_3_), channel_id=1, source_target_pairs={{0,2},{2,0},{1,3},{3,1},{4,6},{6,4},{5,7},{7,5},{8,10},{10,8},{9,1... | collective-permute-start | bytes 2457608 | tf_op jit(solution)/shard_map/ppermute | solution.py:234
  100.5 33.8 %collective-permute-start.13 = (bf16[4,16,6400]{2,1,0:T(8,128)(2,1)S(1)}, bf16[4,16,6400]{2,1,0:T(8,128)(2,1)}, u32[]{:S(2)}, u32[]{:S(2)}) collective-permute-start(bf16[4,16,6400]{2,1,0:T(8,128)(2,1)S(1)} %pad_maximum_fusion.3), channel_id=1, source_target_pairs={{0,1},{1,0},{2,3},{3,2},{4,5},{5,4},{6,7},{7,6},{8,9},{9,8},{10,11... | collective-permute-start | bytes 2457608 | tf_op jit(solution)/shard_map/ppermute | solution.py:234
  101.1 35.7 %collective-permute-start.14 = (bf16[4,16,6400]{2,1,0:T(8,128)(2,1)S(1)}, bf16[4,16,6400]{2,1,0:T(8,128)(2,1)}, u32[]{:S(2)}, u32[]{:S(2)}) collective-permute-start(bf16[4,16,6400]{2,1,0:T(8,128)(2,1)S(1)} %pad_maximum_fusion.4), channel_id=1, source_target_pairs={{0,4},{4,0},{1,5},{5,1},{2,6},{6,2},{3,7},{7,3},{8,12},{12,8},{9,1... | collective-permute-start | bytes 2457608 | tf_op jit(solution)/shard_map/ppermute | solution.py:234
  139.3 23.6 %collective-permute-start.16 = (bf16[2,2,16,2688]{3,2,0,1:T(8,128)(2,1)S(1)}, bf16[2,2,16,2688]{3,2,0,1:T(8,128)(2,1)S(1)}, u32[]{:S(2)}, u32[]{:S(2)}) collective-permute-start(bf16[2,2,16,2688]{3,2,0,1:T(8,128)(2,1)S(1)} %pad_maximum_fusion.15), channel_id=1, source_target_pairs={{0,8},{8,0},{1,9},{9,1},{2,10},{10,2},{3,11},{11,3},{4,12},{12,4},... | collective-permute-start | bytes 1032200 | tf_op jit(solution)/shard_map/ppermute | solution.py:234
  140.0 44.4 %collective-permute-start.17 = (bf16[8,16,6400]{2,1,0:T(8,128)(2,1)}, bf16[8,16,6400]{2,1,0:T(8,128)(2,1)}, u32[]{:S(2)}, u32[]{:S(2)}) collective-permute-start(bf16[8,16,6400]{2,1,0:T(8,128)(2,1)} %pad_maximum_fusion.refs_0_), channel_id=1, source_target_pairs={{0,4},{4,0},{1,5},{5,1},{2,6},{6,2},{3,7},{7,3},{8,12},{12,8},{9,1... | collective-permute-start | bytes 4915208 | tf_op jit(solution)/shard_map/ppermute | solution.py:234
  140.8 43.5 %collective-permute-start.18 = (bf16[8,16,6400]{2,1,0:T(8,128)(2,1)}, bf16[8,16,6400]{2,1,0:T(8,128)(2,1)}, u32[]{:S(2)}, u32[]{:S(2)}) collective-permute-start(bf16[8,16,6400]{2,1,0:T(8,128)(2,1)} %pad_maximum_fusion.1.refs_2_), channel_id=1, source_target_pairs={{0,1},{1,0},{2,3},{3,2},{4,5},{5,4},{6,7},{7,6},{8,9},{9,8},{10,11... | collective-permute-start | bytes 4915208 | tf_op jit(solution)/shard_map/ppermute | solution.py:234
  184.5 23.1 %collective-permute-start.22 = (bf16[8,16,6400]{2,1,0:T(8,128)(2,1)}, bf16[8,16,6400]{2,1,0:T(8,128)(2,1)}, u32[]{:S(2)}, u32[]{:S(2)}) collective-permute-start(bf16[8,16,6400]{2,1,0:T(8,128)(2,1)} %collective-permute-done.17.refs_1_), channel_id=1, source_target_pairs={{0,2},{2,0},{1,3},{3,1},{4,6},{6,4},{5,7},{7,5},{8,10},{10,8},{9,1... | collective-permute-start | bytes 4915208 | tf_op jit(solution)/shard_map/ppermute | solution.py:234
  185.0 24.1 %collective-permute-start.23 = (bf16[8,16,6400]{2,1,0:T(8,128)(2,1)}, bf16[8,16,6400]{2,1,0:T(8,128)(2,1)}, u32[]{:S(2)}, u32[]{:S(2)}) collective-permute-start(bf16[8,16,6400]{2,1,0:T(8,128)(2,1)} %pad_maximum_fusion.1.refs_2_), channel_id=1, source_target_pairs={{0,2},{2,0},{1,3},{3,1},{4,6},{6,4},{5,7},{7,5},{8,10},{10,8},{9,1... | collective-permute-start | bytes 4915208 | tf_op jit(solution)/shard_map/ppermute | solution.py:234
  185.0 24.0 %collective-permute-start.24 = (bf16[8,16,6400]{2,1,0:T(8,128)(2,1)}, bf16[8,16,6400]{2,1,0:T(8,128)(2,1)}, u32[]{:S(2)}, u32[]{:S(2)}) collective-permute-start(bf16[8,16,6400]{2,1,0:T(8,128)(2,1)} %collective-permute-done.18.refs_3_), channel_id=1, source_target_pairs={{0,2},{2,0},{1,3},{3,1},{4,6},{6,4},{5,7},{7,5},{8,10},{10,8},{9,1... | collective-permute-start | bytes 4915208 | tf_op jit(solution)/shard_map/ppermute | solution.py:234
  204.9 39.5 %collective-permute-start.27 = (bf16[512,1024]{1,0:T(8,128)(2,1)}, bf16[512,1024]{1,0:T(8,128)(2,1)}, u32[]{:S(2)}, u32[]{:S(2)}) collective-permute-start(bf16[512,1024]{1,0:T(8,128)(2,1)} %get-tuple-element.252), channel_id=1, source_target_pairs={{0,1},{1,0},{2,3},{3,2},{4,5},{5,4},{6,7},{7,6},{8,9},{9,8},{10,11... | collective-permute-start | bytes 3145736 | tf_op jit(solution)/shard_map/ppermute | solution.py:234
  207.6 35.8 %collective-permute-start.26 = (bf16[8,16,2688]{2,1,0:T(8,128)(2,1)}, bf16[8,16,2688]{2,1,0:T(8,128)(2,1)}, u32[]{:S(2)}, u32[]{:S(2)}) collective-permute-start(bf16[8,16,2688]{2,1,0:T(8,128)(2,1)} %pad_maximum_fusion.6.refs_2_), channel_id=1, source_target_pairs={{0,1},{1,0},{2,3},{3,2},{4,5},{5,4},{6,7},{7,6},{8,9},{9,8},{10,11... | collective-permute-start | bytes 2064392 | tf_op jit(solution)/shard_map/ppermute | solution.py:234
  337.9 49.5 %collective-permute-start.35 = (bf16[512,5376]{1,0:T(8,128)(2,1)}, bf16[512,5376]{1,0:T(8,128)(2,1)S(1)}, u32[]{:S(2)}, u32[]{:S(2)}) collective-permute-start(bf16[512,5376]{1,0:T(8,128)(2,1)} %get-tuple-element.170), channel_id=1, source_target_pairs={{0,2},{2,0},{1,3},{3,1},{4,6},{6,4},{5,7},{7,5},{8,10},{10,8},{9,1... | collective-permute-start | bytes 16515080 | tf_op jit(solution)/shard_map/ppermute | solution.py:234
  401.9 39.8 %collective-permute-start.39 = (bf16[128,5376]{1,0:T(8,128)(2,1)}, bf16[128,5376]{1,0:T(8,128)(2,1)}, u32[]{:S(2)}, u32[]{:S(2)}) collective-permute-start(bf16[128,5376]{1,0:T(8,128)(2,1)} %get-tuple-element.181), channel_id=1, source_target_pairs={{0,4},{4,0},{1,5},{5,1},{2,6},{6,2},{3,7},{7,3},{8,12},{12,8},{9,1... | collective-permute-start | bytes 4128776 | tf_op jit(solution)/shard_map/ppermute | solution.py:234
  403.2 40.9 %collective-permute-start.40 = (bf16[128,5376]{1,0:T(8,128)(2,1)}, bf16[128,5376]{1,0:T(8,128)(2,1)}, u32[]{:S(2)}, u32[]{:S(2)}) collective-permute-start(bf16[128,5376]{1,0:T(8,128)(2,1)} %get-tuple-element.182), channel_id=1, source_target_pairs={{0,1},{1,0},{2,3},{3,2},{4,5},{5,4},{6,7},{7,6},{8,9},{9,8},{10,11... | collective-permute-start | bytes 4128776 | tf_op jit(solution)/shard_map/ppermute | solution.py:234
  423.2 27.4 %collective-permute-start.41 = (bf16[512,1024]{1,0:T(8,128)(2,1)}, bf16[512,1024]{1,0:T(8,128)(2,1)}, u32[]{:S(2)}, u32[]{:S(2)}) collective-permute-start(bf16[512,1024]{1,0:T(8,128)(2,1)} %get-tuple-element.185), channel_id=1, source_target_pairs={{0,2},{2,0},{1,3},{3,1},{4,6},{6,4},{5,7},{7,5},{8,10},{10,8},{9,1... | collective-permute-start | bytes 3145736 | tf_op jit(solution)/shard_map/ppermute | solution.py:234
  446.8 29.2 %collective-permute-start.42 = (bf16[64,5376]{1,0:T(8,128)(2,1)}, bf16[64,5376]{1,0:T(8,128)(2,1)S(1)}, u32[]{:S(2)}, u32[]{:S(2)}) collective-permute-start(bf16[64,5376]{1,0:T(8,128)(2,1)} %get-tuple-element.187), channel_id=1, source_target_pairs={{0,1},{1,0},{2,3},{3,2},{4,5},{5,4},{6,7},{7,6},{8,9},{9,8},{10,11... | collective-permute-start | bytes 2064392 | tf_op jit(solution)/shard_map/ppermute | solution.py:234
  449.0 27.1 %collective-permute-start.43 = (bf16[64,5376]{1,0:T(8,128)(2,1)}, bf16[64,5376]{1,0:T(8,128)(2,1)S(1)}, u32[]{:S(2)}, u32[]{:S(2)}) collective-permute-start(bf16[64,5376]{1,0:T(8,128)(2,1)} %get-tuple-element.188), channel_id=1, source_target_pairs={{0,4},{4,0},{1,5},{5,1},{2,6},{6,2},{3,7},{7,3},{8,12},{12,8},{9,1... | collective-permute-start | bytes 2064392 | tf_op jit(solution)/shard_map/ppermute | solution.py:234
  527.5 27.6 %collective-permute-start.51 = (bf16[512,3072]{1,0:T(8,128)(2,1)}, bf16[512,3072]{1,0:T(8,128)(2,1)S(1)}, u32[]{:S(2)}, u32[]{:S(2)}) collective-permute-start(bf16[512,3072]{1,0:T(8,128)(2,1)} %get-tuple-element.206), channel_id=1, source_target_pairs={{0,2},{2,0},{1,3},{3,1},{4,6},{6,4},{5,7},{7,5},{8,10},{10,8},{9,1... | collective-permute-start | bytes 9437192 | tf_op jit(solution)/shard_map/ppermute | solution.py:234
  530.5 48.2 %collective-permute-start.46 = (bf16[512,1024]{1,0:T(8,128)(2,1)S(1)}, bf16[512,1024]{1,0:T(8,128)(2,1)S(1)}, u32[]{:S(2)}, u32[]{:S(2)}) collective-permute-start(bf16[512,1024]{1,0:T(8,128)(2,1)S(1)} %get-tuple-element.246), channel_id=1, source_target_pairs={{0,1},{1,0},{2,3},{3,2},{4,5},{5,4},{6,7},{7,6},{8,9},{9,8},{10,11... | collective-permute-start | bytes 3145736 | tf_op jit(solution)/shard_map/ppermute | solution.py:234
  (90 other events, 1336.7 us)

commit v2 on v1

--- a/solution.py
+++ b/solution.py
@@ -650,15 +650,16 @@
     one.go()
     rows_in = whole_rows(tokens, place)
     one.go()
-    shard_two, shard_three, cotangent = one.go(shard_two, shard_three, cotangent)
+    shard_two = one.go(shard_two)
     two = Chain(gather_steps(shard_two))
     two.go()
     one.go()
+    cotangent, two.waiting = one.go(cotangent, two.waiting)
+    grad_low = whole_rows(cotangent, place)
     two.go()
-    one.go()
     full_qkv = assemble(one.value, coords, 3072, 1024, 0)
     gain_cols = assemble(one.value, coords, 128, 128, 24)
-    shard_three, cotangent = two.go(shard_three, cotangent)
+    full_qkv, shard_three = two.go(full_qkv, shard_three)
     three = Chain(gather_steps(shard_three))
     three.go()
     gain_rows = gain_cols[:, :2].astype(F32).T
@@ -667,13 +668,12 @@
     first, qkv = qkv_call(rows_in, full_one, full_qkv, cosine, sine)
     qkv = two.go(qkv)
     qkv = three.go(qkv)
-    halves = attend_call(qkv, 0, 4, None)
+    halves = attend_call(qkv, 0, 3, None)
     halves = three.go(*halves)
-    halves, cotangent = barrier((halves, cotangent))
-    grad_low = whole_rows(cotangent, place)
-    attended, lse = attend_call(qkv, 4, 4, halves)
+    halves = attend_call(qkv, 3, 4, halves)
+    halves = three.go(*halves)
+    attended, lse = attend_call(qkv, 7, 1, halves)
     attended = two.go(attended)
-    attended = three.go(attended)
     full_out = assemble(two.value, coords, 1024, 256, 2 * padded // 256)
     full_gate = assemble(two.value, coords, padded, 896, 0)
     full_up = assemble(two.value, coords, padded, 896, padded // 896)
@@ -703,7 +703,6 @@
     d_gate = down.go(d_gate)
     grad_second = nt(d_gate, full_gate)
     grad_second, d_up = feed.go(grad_second, d_up)
-    grad_second, d_up = down.go(grad_second, d_up)
     grad_second = grad_second + nt(d_up, full_up)
     grad_resid, part_two = norm_back(grad_second, normed_two, inverse_two, full_two)
     grad_resid = grad_resid + grad_low.astype(F32)
@@ -715,6 +714,7 @@
         scatter_steps(*grad_call(coords, attended, grad_proj, out_spec, 1024, 512, 1024, 0, None))
     )
     datt = out.go(datt)
+    datt = down.go(datt)
     fused = attend_back_call(qkv, attended, lse, datt, cosine, sine, 0, 2, None)
     fused = feed.go(fused)
     fused = out.go(fused)

time: 627 us -> 610 us (0.973)
  waiting for transfers between devices: 184 us -> 166 us
    ppermute x67, waiting for transfers between devices: 184 us -> 166 us  [swap(): return lax.ppermute(values, axis, [(0, 1), (1, 0)])]
    pallas_call x2 -> x3, Pallas kernels: 41.1 us -> 43.1 us  [attend_call(): pl.pallas_call(attend_kernel, grid=(count,), out_shape=[jax.ShapeDtypeStr...]
  transfers between devices with their start and end apart: 67 -> 67, of which waited for: 27 -> 28; matrix products, arithmetic and copies ran while one was open for 17% -> 16% of each run, Pallas kernels for 28% -> 28%
where the time goes in v2:
time: 610 us; the launch traced here: 606 us
  Pallas kernels  245 us (40%)
  waiting for transfers between devices  166 us (27%)
  other arithmetic  64.5 us (11%)
  starting transfers between devices  63.8 us (10%)
  matrix products  50.1 us (8%)
  local copies, waits for them, and re-layouts  14.5 us (2%)
    ppermute x67, waiting for transfers between devices, swap(): return lax.ppermute(values, axis, [(0, 1), (1, 0)])  166 us
    pallas_call x4, Pallas kernels, attend_back_call(): pl.pallas_call(attend_back_kernel, grid=(count,), out_shape=jax.ShapeDtyp...  67.4 us
    ppermute x67, starting transfers between devices, swap(): return lax.ppermute(values, axis, [(0, 1), (1, 0)])  63.8 us
    pallas_call x5, Pallas kernels, grad_call(): pl.pallas_call(grad_kernel, grid=(steps,), out_shape=[jax.ShapeDtypeStruc...  54.4 us
    dot_general x7, matrix products, nt(): lax.dot_general(left, right, (((1,), (1,)), ((), ())), preferred_element_...  45.5 us
    pallas_call x3, Pallas kernels, attend_call(): pl.pallas_call(attend_kernel, grid=(count,), out_shape=[jax.ShapeDtypeStr...  43.1 us
    pallas_call x6, Pallas kernels, assemble(): pl.pallas_call(assemble_kernel, grid=(width // block,), out_shape=jax.Sha...  31 us
    pallas_call x1, Pallas kernels, feed_call(): pl.pallas_call(feed_kernel, grid=(width // block,), out_shape=[jax.ShapeD...  29.4 us
  transfers between devices with their start and end apart: 67, of which 28 were waited for; matrix products, arithmetic and copies ran while one was open for 16% of the time, Pallas kernels for 28%

profile of v2, /device:TPU:0, one launch (start us, length us, event | category | flops | bytes accessed | tf_op | source)
XLA Modules:
  0.0 605.6 jit_solution(2726737380665467332)
XLA Ops:
  17.8 9.0 %collective-permute-done.2 = bf16[2,2,16,3200]{3,2,0,1:T(8,128)(2,1)S(1)} collective-permute-done((bf16[2,2,16,3200]{3,2,0,1:T(8,128)(2,1)S(1)}, bf16[2,2,16,3200]{3,2,0,1:T(8,128)(2,1)S(1)}, u32[]{:S(2)}, u32[]{:S(2)}) %collective-permute-start.2) | collective-permute-done | bytes 409632 | tf_op jit(solution)/shard_map/ppermute | solution.py:234
  33.2 8.8 %collective-permute-done.6 = bf16[4,16,3200]{2,1,0:T(8,128)(2,1)S(1)} collective-permute-done((bf16[4,16,3200]{2,1,0:T(8,128)(2,1)S(1)}, bf16[4,16,3200]{2,1,0:T(8,128)(2,1)S(1)}, u32[]{:S(2)}, u32[]{:S(2)}) %collective-permute-start.6) | collective-permute-done | bytes 409632 | tf_op jit(solution)/shard_map/ppermute | solution.py:234
  64.5 15.3 %collective-permute-done.12 = bf16[2,2,16,6400]{3,2,0,1:T(8,128)(2,1)S(1)} collective-permute-done((bf16[2,2,16,6400]{3,2,0,1:T(8,128)(2,1)S(1)}, bf16[2,2,16,6400]{3,2,0,1:T(8,128)(2,1)S(1)}, u32[]{:S(2)}, u32[]{:S(2)}) %collective-permute-start.12) | collective-permute-done | bytes 819232 | tf_op jit(solution)/shard_map/ppermute | solution.py:234
  94.9 19.7 %norm_qkv.1 = (bf16[1024,1024]{1,0:T(8,128)(2,1)}, bf16[1024,3072]{1,0:T(8,128)(2,1)}) custom-call(bf16[1024,1024]{1,0:T(8,128)(2,1)} %get-tuple-element.230.tok_ref, f32[1,1024]{1,0:T(1,128)} %get-tuple-element.305.gain_ref, bf16[1024,3072]{1,0:T(8,128)(2,1)} %assemble.7.w_ref, f32[1024,128]{1,0:T(8,128)} %get-tuple-element.314.cos_ref, ...), custom_call_target="tpu_custom_call" | custom-call | flops 14000000000 | bytes 20000000 | tf_op jit(solution)/shard_map/norm_qkv/pallas_call | solution.py:443
  121.7 15.9 %attend.3 = (bf16[1024,1024]{1,0:T(8,128)(2,1)}, f32[1024,1024]{1,0:T(8,128)}) custom-call(bf16[1024,3072]{1,0:T(8,128)(2,1)} %get-tuple-element.130.q_ref.k_ref.v_ref, bf16[1024,3072]{1,0:T(8,128)(2,1)} %get-tuple-element.130.q_ref.k_ref.v_ref, bf16[1024,3072]{1,0:T(8,128)(2,1)} %get-tuple-element.130.q_ref.k_ref.v_ref), custom_call_target="tpu_custom_call" | custom-call | flops 10499999744 | bytes 15000000 | tf_op jit(solution)/shard_map/attend/pallas_call | solution.py:497
  140.1 20.5 %attend.4 = (bf16[1024,1024]{1,0:T(8,128)(2,1)}, f32[1024,1024]{1,0:T(8,128)}) custom-call(bf16[1024,3072]{1,0:T(8,128)(2,1)} %get-tuple-element.130.q_ref.k_ref.v_ref, bf16[1024,3072]{1,0:T(8,128)(2,1)} %get-tuple-element.130.q_ref.k_ref.v_ref, ...), custom_call_target="tpu_custom_call", output_to_operand_aliasing={{0}: (3, {}), {1}: (4, {})} | custom-call | flops 14000000000 | bytes 20000000 | tf_op jit(solution)/shard_map/attend/pallas_call | solution.py:497
  192.0 19.9 %collective-permute-done.26.refs_3_ = bf16[8,16,2688]{2,1,0:T(8,128)(2,1)} collective-permute-done((bf16[8,16,2688]{2,1,0:T(8,128)(2,1)}, bf16[8,16,2688]{2,1,0:T(8,128)(2,1)}, u32[]{:S(2)}, u32[]{:S(2)}) %collective-permute-start.26) | collective-permute-done | bytes 688160 | tf_op jit(solution)/shard_map/ppermute | solution.py:234
  236.7 29.4 %feed.1 = (bf16[1024,2688]{1,0:T(8,128)(2,1)}, bf16[1024,2688]{1,0:T(8,128)(2,1)}, bf16[1024,2688]{1,0:T(8,128)(2,1)}) custom-call(bf16[1024,1024]{1,0:T(8,128)(2,1)} %multiply_convert_fusion.second_ref.x_ref, bf16[1024,1024]{1,0:T(8,128)(2,1)} %maximum_select_fusion.1.grad_ref.x_ref, bf16[1024,2688]{1,0:T(8,128)(2,1)} %assemble.9.gate_ref, ...), custom_call_target="tpu_custom_call" | custom-call | flops 20999999488 | bytes 30000000 | tf_op jit(solution)/shard_map/feed/pallas_call | solution.py:605
  266.1 11.8 %weight_grad.5 = (bf16[512,2688]{1,0:T(8,128)(2,1)}, bf16[512,2688]{1,0:T(8,128)(2,1)}) custom-call(s32[5]{0:T(128)} %stack.111.coords, bf16[1024,1024]{1,0:T(8,128)(2,1)} %maximum_select_fusion.1.grad_ref.x_ref, bf16[1024,2688]{1,0:T(8,128)(2,1)} %get-tuple-element.160.y_ref), custom_call_target="tpu_custom_call" | custom-call | flops 8180869632 | bytes 11686956 | tf_op jit(solution)/shard_map/weight_grad/pallas_call | solution.py:349
  279.2 12.0 %weight_grad.6 = (bf16[512,5376]{1,0:T(8,128)(2,1)}, bf16[512,5376]{1,0:T(8,128)(2,1)}) custom-call(s32[5]{0:T(128)} %stack.111.coords, bf16[1024,1024]{1,0:T(8,128)(2,1)} %multiply_convert_fusion.second_ref.x_ref, bf16[1024,2688]{1,0:T(8,128)(2,1)} %get-tuple-element.175.y_ref), custom_call_target="tpu_custom_call" | custom-call | flops 8180869632 | bytes 11686956 | tf_op jit(solution)/shard_map/weight_grad/pallas_call | solution.py:349
  294.7 11.9 %weight_grad.7 = (bf16[512,5376]{1,0:T(8,128)(2,1)}, bf16[512,5376]{1,0:T(8,128)(2,1)}) custom-call(s32[5]{0:T(128)} %stack.111.coords, bf16[1024,1024]{1,0:T(8,128)(2,1)} %multiply_convert_fusion.second_ref.x_ref, bf16[1024,2688]{1,0:T(8,128)(2,1)} %get-tuple-element.179.y_ref, ...), custom_call_target="tpu_custom_call", output_to_operand_aliasing={{0}: (3, {}), {1}: (4, {})} | custom-call | flops 8180869632 | bytes 11686956 | tf_op jit(solution)/shard_map/weight_grad/pallas_call | solution.py:349
  308.4 11.5 %add_convert_fusion = bf16[1024,1024]{1,0:T(8,128)(2,1)} fusion(f32[1024,1024]{1,0:T(8,128)} %copy-done, bf16[1024,2688]{1,0:T(8,128)(2,1)} %get-tuple-element.160.y_ref, bf16[1024,2688]{1,0:T(8,128)(2,1)} %assemble.11.down_ref), kind=kOutput, calls=%fused_computation.17 | convolution fusion | flops 5639241728 | bytes 17301504 | tf_op jit(solution)/shard_map/dot_general | solution.py:238
  324.6 12.9 %collective-permute-done.34 = bf16[128,2688]{1,0:T(8,128)(2,1)S(1)} collective-permute-done((bf16[128,2688]{1,0:T(8,128)(2,1)S(1)}, bf16[128,2688]{1,0:T(8,128)(2,1)S(1)}, u32[]{:S(2)}, u32[]{:S(2)}) %collective-permute-start.34) | collective-permute-done | bytes 688160 | tf_op jit(solution)/shard_map/ppermute | solution.py:234
  339.5 8.3 %fusion.64 = f32[1024,1024]{1,0:T(8,128)S(1)} fusion(bf16[1024,2688]{1,0:T(8,128)(2,1)} %get-tuple-element.175.y_ref, bf16[1024,2688]{1,0:T(8,128)(2,1)S(1)} %bitcast.190), kind=kOutput, calls=%fused_computation.221 | convolution fusion | flops 5637144576 | bytes 15204352 | tf_op jit(solution)/shard_map/dot_general | solution.py:238
  348.6 8.7 %collective-permute-done.37 = bf16[64,2688]{1,0:T(8,128)(2,1)S(1)} collective-permute-done((bf16[64,2688]{1,0:T(8,128)(2,1)S(1)}, bf16[64,2688]{1,0:T(8,128)(2,1)S(1)}, u32[]{:S(2)}, u32[]{:S(2)}) %collective-permute-start.37) | collective-permute-done | bytes 344096 | tf_op jit(solution)/shard_map/ppermute | solution.py:234
  359.9 8.3 %fusion.65 = f32[1024,1024]{1,0:T(8,128)S(1)} fusion(bf16[1024,2688]{1,0:T(8,128)(2,1)} %get-tuple-element.179.y_ref, bf16[1024,2688]{1,0:T(8,128)(2,1)S(1)} %bitcast.188), kind=kOutput, calls=%fused_computation.222 | convolution fusion | flops 5637144576 | bytes 15204352 | tf_op jit(solution)/shard_map/dot_general | solution.py:238
  390.3 16.8 %attend_back.4.refs_0_ = bf16[3,1024,1024]{2,1,0:T(8,128)(2,1)} custom-call(bf16[1024,3072]{1,0:T(8,128)(2,1)} %get-tuple-element.130.q_ref.k_ref.v_ref, bf16[1024,3072]{1,0:T(8,128)(2,1)} %get-tuple-element.130.q_ref.k_ref.v_ref, bf16[1024,3072]{1,0:T(8,128)(2,1)} %get-tuple-element.130.q_ref.k_ref.v_ref, ...), custom_call_target="tpu_custom_call" | custom-call | flops 10499999744 | bytes 15000000 | tf_op jit(solution)/shard_map/attend_back/pallas_call | solution.py:565
  427.0 16.8 %attend_back.5.refs_0_ = bf16[3,1024,1024]{2,1,0:T(8,128)(2,1)} custom-call(bf16[1024,3072]{1,0:T(8,128)(2,1)} %get-tuple-element.130.q_ref.k_ref.v_ref, bf16[1024,3072]{1,0:T(8,128)(2,1)} %get-tuple-element.130.q_ref.k_ref.v_ref, bf16[1024,3072]{1,0:T(8,128)(2,1)} %get-tuple-element.130.q_ref.k_ref.v_ref, ...), custom_call_target="tpu_custom_call", output_to_operand_aliasing={{}: (8, {})} | custom-call | flops 10499999744 | bytes 15000000 | tf_op jit(solution)/shard_map/attend_back/pallas_call | solution.py:565
  448.6 11.5 %collective-permute-done.43 = bf16[64,5376]{1,0:T(8,128)(2,1)S(1)} collective-permute-done((bf16[64,5376]{1,0:T(8,128)(2,1)S(1)}, bf16[64,5376]{1,0:T(8,128)(2,1)S(1)}, u32[]{:S(2)}, u32[]{:S(2)}) %collective-permute-start.43) | collective-permute-done | bytes 688160 | tf_op jit(solution)/shard_map/ppermute | solution.py:234
  462.4 17.0 %attend_back.6.refs_0_ = bf16[3,1024,1024]{2,1,0:T(8,128)(2,1)} custom-call(bf16[1024,3072]{1,0:T(8,128)(2,1)} %get-tuple-element.130.q_ref.k_ref.v_ref, bf16[1024,3072]{1,0:T(8,128)(2,1)} %get-tuple-element.130.q_ref.k_ref.v_ref, bf16[1024,3072]{1,0:T(8,128)(2,1)} %get-tuple-element.130.q_ref.k_ref.v_ref, ...), custom_call_target="tpu_custom_call", output_to_operand_aliasing={{}: (8, {})} | custom-call | flops 10499999744 | bytes 15000000 | tf_op jit(solution)/shard_map/attend_back/pallas_call | solution.py:565
  481.8 16.8 %attend_back.7.y_ref = bf16[3,1024,1024]{2,1,0:T(8,128)(2,1)} custom-call(bf16[1024,3072]{1,0:T(8,128)(2,1)} %get-tuple-element.130.q_ref.k_ref.v_ref, bf16[1024,3072]{1,0:T(8,128)(2,1)} %get-tuple-element.130.q_ref.k_ref.v_ref, bf16[1024,3072]{1,0:T(8,128)(2,1)} %get-tuple-element.130.q_ref.k_ref.v_ref, ...), custom_call_target="tpu_custom_call", output_to_operand_aliasing={{}: (8, {})} | custom-call | flops 10499999744 | bytes 15000000 | tf_op jit(solution)/shard_map/attend_back/pallas_call | solution.py:565
  498.7 12.3 %weight_grad.9 = (bf16[512,3072]{1,0:T(8,128)(2,1)}, bf16[512,3072]{1,0:T(8,128)(2,1)}) custom-call(s32[5]{0:T(128)} %stack.111.coords, bf16[1024,1024]{1,0:T(8,128)(2,1)} %get-tuple-element.208.x_ref, bf16[3,1024,1024]{2,1,0:T(8,128)(2,1)} %attend_back.7.y_ref), custom_call_target="tpu_custom_call" | custom-call | flops 9349565440 | bytes 13356521 | tf_op jit(solution)/shard_map/weight_grad/pallas_call | solution.py:349
  523.4 13.7 %collective-permute-done.59 = bf16[2,16,1024]{2,1,0:T(8,128)(2,1)S(1)} collective-permute-done((bf16[2,16,1024]{2,1,0:T(8,128)(2,1)S(1)}, bf16[2,16,1024]{2,1,0:T(8,128)(2,1)S(1)}, u32[]{:S(2)}, u32[]{:S(2)}) %collective-permute-start.59) | collective-permute-done | bytes 65568 | tf_op jit(solution)/shard_map/ppermute | solution.py:234
  550.7 8.8 %collective-permute-done.52 = bf16[128,3072]{1,0:T(8,128)(2,1)S(1)} collective-permute-done((bf16[128,3072]{1,0:T(8,128)(2,1)S(1)}, bf16[128,3072]{1,0:T(8,128)(2,1)S(1)}, u32[]{:S(2)}, u32[]{:S(2)}) %collective-permute-start.52) | collective-permute-done | bytes 786464 | tf_op jit(solution)/shard_map/ppermute | solution.py:234
  (348 shorter events, 266.0 us)
Async XLA Ops:
  9.3 41.4 %collective-permute-start = (bf16[512,1024]{1,0:T(8,128)(2,1)}, bf16[512,1024]{1,0:T(8,128)(2,1)}, u32[]{:S(2)}, u32[]{:S(2)}) collective-permute-start(bf16[512,1024]{1,0:T(8,128)(2,1)} %get-tuple-element.260), channel_id=1, source_target_pairs={{0,1},{1,0},{2,3},{3,2},{4,5},{5,4},{6,7},{7,6},{8,9},{9,8},{10,11... | collective-permute-start | bytes 3145736 | tf_op jit(solution)/shard_map/ppermute | solution.py:234
  28.3 21.3 %collective-permute-start.3 = (bf16[2,16,6400]{2,1,0:T(8,128)(2,1)}, bf16[2,16,6400]{2,1,0:T(8,128)(2,1)S(1)}, u32[]{:S(2)}, u32[]{:S(2)}) collective-permute-start(bf16[2,16,6400]{2,1,0:T(8,128)(2,1)} %bitcast.17), channel_id=1, source_target_pairs={{0,16},{16,0},{1,17},{17,1},{2,18},{18,2},{3,19},{19,3},{4,20},{20... | collective-permute-start | bytes 1228808 | tf_op jit(solution)/shard_map/ppermute | solution.py:234
  88.7 26.0 %collective-permute-start.15 = (bf16[2,16,2688]{2,1,0:T(8,128)(2,1)S(1)}, bf16[2,16,2688]{2,1,0:T(8,128)(2,1)S(1)}, u32[]{:S(2)}, u32[]{:S(2)}) collective-permute-start(bf16[2,16,2688]{2,1,0:T(8,128)(2,1)S(1)} %bitcast.216), channel_id=1, source_target_pairs={{0,16},{16,0},{1,17},{17,1},{2,18},{18,2},{3,19},{19,3},{4,20},{20... | collective-permute-start | bytes 516104 | tf_op jit(solution)/shard_map/ppermute | solution.py:234
  93.1 21.6 %collective-permute-start.13 = (bf16[4,16,6400]{2,1,0:T(8,128)(2,1)S(1)}, bf16[4,16,6400]{2,1,0:T(8,128)(2,1)}, u32[]{:S(2)}, u32[]{:S(2)}) collective-permute-start(bf16[4,16,6400]{2,1,0:T(8,128)(2,1)S(1)} %pad_maximum_fusion.3), channel_id=1, source_target_pairs={{0,1},{1,0},{2,3},{3,2},{4,5},{5,4},{6,7},{7,6},{8,9},{9,8},{10,11... | collective-permute-start | bytes 2457608 | tf_op jit(solution)/shard_map/ppermute | solution.py:234
  93.4 23.8 %collective-permute-start.14 = (bf16[4,16,6400]{2,1,0:T(8,128)(2,1)S(1)}, bf16[4,16,6400]{2,1,0:T(8,128)(2,1)S(1)}, u32[]{:S(2)}, u32[]{:S(2)}) collective-permute-start(bf16[4,16,6400]{2,1,0:T(8,128)(2,1)S(1)} %pad_maximum_fusion.4), channel_id=1, source_target_pairs={{0,4},{4,0},{1,5},{5,1},{2,6},{6,2},{3,7},{7,3},{8,12},{12,8},{9,1... | collective-permute-start | bytes 2457608 | tf_op jit(solution)/shard_map/ppermute | solution.py:234
  120.0 49.4 %collective-permute-start.19 = (bf16[8,16,6400]{2,1,0:T(8,128)(2,1)}, bf16[8,16,6400]{2,1,0:T(8,128)(2,1)}, u32[]{:S(2)}, u32[]{:S(2)}) collective-permute-start(bf16[8,16,6400]{2,1,0:T(8,128)(2,1)} %pad_maximum_fusion.refs_0_), channel_id=1, source_target_pairs={{0,4},{4,0},{1,5},{5,1},{2,6},{6,2},{3,7},{7,3},{8,12},{12,8},{9,1... | collective-permute-start | bytes 4915208 | tf_op jit(solution)/shard_map/ppermute | solution.py:234
  120.5 48.9 %collective-permute-start.20 = (bf16[8,16,6400]{2,1,0:T(8,128)(2,1)}, bf16[8,16,6400]{2,1,0:T(8,128)(2,1)}, u32[]{:S(2)}, u32[]{:S(2)}) collective-permute-start(bf16[8,16,6400]{2,1,0:T(8,128)(2,1)} %pad_maximum_fusion.1.refs_2_), channel_id=1, source_target_pairs={{0,1},{1,0},{2,3},{3,2},{4,5},{5,4},{6,7},{7,6},{8,9},{9,8},{10,11... | collective-permute-start | bytes 4915208 | tf_op jit(solution)/shard_map/ppermute | solution.py:234
  137.8 23.0 %collective-permute-start.17 = (bf16[4,16,2688]{2,1,0:T(8,128)(2,1)S(1)}, bf16[4,16,2688]{2,1,0:T(8,128)(2,1)S(1)}, u32[]{:S(2)}, u32[]{:S(2)}) collective-permute-start(bf16[4,16,2688]{2,1,0:T(8,128)(2,1)S(1)} %pad_maximum_fusion.16), channel_id=1, source_target_pairs={{0,1},{1,0},{2,3},{3,2},{4,5},{5,4},{6,7},{7,6},{8,9},{9,8},{10,11... | collective-permute-start | bytes 1032200 | tf_op jit(solution)/shard_map/ppermute | solution.py:234
  138.6 23.1 %collective-permute-start.18 = (bf16[4,16,2688]{2,1,0:T(8,128)(2,1)S(1)}, bf16[4,16,2688]{2,1,0:T(8,128)(2,1)S(1)}, u32[]{:S(2)}, u32[]{:S(2)}) collective-permute-start(bf16[4,16,2688]{2,1,0:T(8,128)(2,1)S(1)} %pad_maximum_fusion.17), channel_id=1, source_target_pairs={{0,4},{4,0},{1,5},{5,1},{2,6},{6,2},{3,7},{7,3},{8,12},{12,8},{9,1... | collective-permute-start | bytes 1032200 | tf_op jit(solution)/shard_map/ppermute | solution.py:234
  171.6 41.2 %collective-permute-start.27 = (bf16[512,1024]{1,0:T(8,128)(2,1)}, bf16[512,1024]{1,0:T(8,128)(2,1)}, u32[]{:S(2)}, u32[]{:S(2)}) collective-permute-start(bf16[512,1024]{1,0:T(8,128)(2,1)} %get-tuple-element.259), channel_id=1, source_target_pairs={{0,1},{1,0},{2,3},{3,2},{4,5},{5,4},{6,7},{7,6},{8,9},{9,8},{10,11... | collective-permute-start | bytes 3145736 | tf_op jit(solution)/shard_map/ppermute | solution.py:234
  175.6 36.2 %collective-permute-start.26 = (bf16[8,16,2688]{2,1,0:T(8,128)(2,1)}, bf16[8,16,2688]{2,1,0:T(8,128)(2,1)}, u32[]{:S(2)}, u32[]{:S(2)}) collective-permute-start(bf16[8,16,2688]{2,1,0:T(8,128)(2,1)} %pad_maximum_fusion.6.refs_2_), channel_id=1, source_target_pairs={{0,1},{1,0},{2,3},{3,2},{4,5},{5,4},{6,7},{7,6},{8,9},{9,8},{10,11... | collective-permute-start | bytes 2064392 | tf_op jit(solution)/shard_map/ppermute | solution.py:234
  308.2 49.3 %collective-permute-start.35 = (bf16[512,5376]{1,0:T(8,128)(2,1)}, bf16[512,5376]{1,0:T(8,128)(2,1)S(1)}, u32[]{:S(2)}, u32[]{:S(2)}) collective-permute-start(bf16[512,5376]{1,0:T(8,128)(2,1)} %get-tuple-element.177), channel_id=1, source_target_pairs={{0,2},{2,0},{1,3},{3,1},{4,6},{6,4},{5,7},{7,5},{8,10},{10,8},{9,1... | collective-permute-start | bytes 16515080 | tf_op jit(solution)/shard_map/ppermute | solution.py:234
  386.1 22.7 %collective-permute-start.41 = (bf16[512,1024]{1,0:T(8,128)(2,1)}, bf16[512,1024]{1,0:T(8,128)(2,1)}, u32[]{:S(2)}, u32[]{:S(2)}) collective-permute-start(bf16[512,1024]{1,0:T(8,128)(2,1)} %get-tuple-element.191), channel_id=1, source_target_pairs={{0,2},{2,0},{1,3},{3,1},{4,6},{6,4},{5,7},{7,5},{8,10},{10,8},{9,1... | collective-permute-start | bytes 3145736 | tf_op jit(solution)/shard_map/ppermute | solution.py:234
  386.1 32.9 %collective-permute-start.39 = (bf16[128,5376]{1,0:T(8,128)(2,1)}, bf16[128,5376]{1,0:T(8,128)(2,1)}, u32[]{:S(2)}, u32[]{:S(2)}) collective-permute-start(bf16[128,5376]{1,0:T(8,128)(2,1)} %get-tuple-element.187), channel_id=1, source_target_pairs={{0,4},{4,0},{1,5},{5,1},{2,6},{6,2},{3,7},{7,3},{8,12},{12,8},{9,1... | collective-permute-start | bytes 4128776 | tf_op jit(solution)/shard_map/ppermute | solution.py:234
  387.1 34.4 %collective-permute-start.40 = (bf16[128,5376]{1,0:T(8,128)(2,1)}, bf16[128,5376]{1,0:T(8,128)(2,1)}, u32[]{:S(2)}, u32[]{:S(2)}) collective-permute-start(bf16[128,5376]{1,0:T(8,128)(2,1)} %get-tuple-element.188), channel_id=1, source_target_pairs={{0,1},{1,0},{2,3},{3,2},{4,5},{5,4},{6,7},{7,6},{8,9},{9,8},{10,11... | collective-permute-start | bytes 4128776 | tf_op jit(solution)/shard_map/ppermute | solution.py:234
  424.0 20.9 %collective-permute-start.44 = (bf16[128,1024]{1,0:T(8,128)(2,1)}, bf16[128,1024]{1,0:T(8,128)(2,1)}, u32[]{:S(2)}, u32[]{:S(2)}) collective-permute-start(bf16[128,1024]{1,0:T(8,128)(2,1)} %get-tuple-element.196), channel_id=1, source_target_pairs={{0,4},{4,0},{1,5},{5,1},{2,6},{6,2},{3,7},{7,3},{8,12},{12,8},{9,1... | collective-permute-start | bytes 786440 | tf_op jit(solution)/shard_map/ppermute | solution.py:234
  425.0 21.7 %collective-permute-start.45 = (bf16[128,1024]{1,0:T(8,128)(2,1)}, bf16[128,1024]{1,0:T(8,128)(2,1)}, u32[]{:S(2)}, u32[]{:S(2)}) collective-permute-start(bf16[128,1024]{1,0:T(8,128)(2,1)} %get-tuple-element.197), channel_id=1, source_target_pairs={{0,1},{1,0},{2,3},{3,2},{4,5},{5,4},{6,7},{7,6},{8,9},{9,8},{10,11... | collective-permute-start | bytes 786440 | tf_op jit(solution)/shard_map/ppermute | solution.py:234
  425.0 23.4 %collective-permute-start.42 = (bf16[64,5376]{1,0:T(8,128)(2,1)}, bf16[64,5376]{1,0:T(8,128)(2,1)S(1)}, u32[]{:S(2)}, u32[]{:S(2)}) collective-permute-start(bf16[64,5376]{1,0:T(8,128)(2,1)} %get-tuple-element.193), channel_id=1, source_target_pairs={{0,1},{1,0},{2,3},{3,2},{4,5},{5,4},{6,7},{7,6},{8,9},{9,8},{10,11... | collective-permute-start | bytes 2064392 | tf_op jit(solution)/shard_map/ppermute | solution.py:234
  511.0 27.8 %collective-permute-start.51 = (bf16[512,3072]{1,0:T(8,128)(2,1)}, bf16[512,3072]{1,0:T(8,128)(2,1)S(1)}, u32[]{:S(2)}, u32[]{:S(2)}) collective-permute-start(bf16[512,3072]{1,0:T(8,128)(2,1)} %get-tuple-element.212), channel_id=1, source_target_pairs={{0,2},{2,0},{1,3},{3,1},{4,6},{6,4},{5,7},{7,5},{8,10},{10,8},{9,1... | collective-permute-start | bytes 9437192 | tf_op jit(solution)/shard_map/ppermute | solution.py:234
  514.1 48.2 %collective-permute-start.46 = (bf16[512,1024]{1,0:T(8,128)(2,1)S(1)}, bf16[512,1024]{1,0:T(8,128)(2,1)S(1)}, u32[]{:S(2)}, u32[]{:S(2)}) collective-permute-start(bf16[512,1024]{1,0:T(8,128)(2,1)S(1)} %get-tuple-element.253), channel_id=1, source_target_pairs={{0,1},{1,0},{2,3},{3,2},{4,5},{5,4},{6,7},{7,6},{8,9},{9,8},{10,11... | collective-permute-start | bytes 3145736 | tf_op jit(solution)/shard_map/ppermute | solution.py:234
  515.9 21.9 %collective-permute-start.60 = (bf16[2,16,5376]{2,1,0:T(8,128)(2,1)S(1)}, bf16[2,16,5376]{2,1,0:T(8,128)(2,1)S(1)}, u32[]{:S(2)}, u32[]{:S(2)}) collective-permute-start(bf16[2,16,5376]{2,1,0:T(8,128)(2,1)S(1)} %copy-done.33), channel_id=1, source_target_pairs={{0,16},{16,0},{1,17},{17,1},{2,18},{18,2},{3,19},{19,3},{4,20},{20... | collective-permute-start | bytes 1032200 | tf_op jit(solution)/shard_map/ppermute | solution.py:234
  517.9 19.2 %collective-permute-start.59 = (bf16[2,16,1024]{2,1,0:T(8,128)(2,1)S(1)}, bf16[2,16,1024]{2,1,0:T(8,128)(2,1)S(1)}, u32[]{:S(2)}, u32[]{:S(2)}) collective-permute-start(bf16[2,16,1024]{2,1,0:T(8,128)(2,1)S(1)} %fusion.55), channel_id=1, source_target_pairs={{0,16},{16,0},{1,17},{17,1},{2,18},{18,2},{3,19},{19,3},{4,20},{20... | collective-permute-start | bytes 196616 | tf_op jit(solution)/shard_map/ppermute | solution.py:234
  540.1 19.4 %collective-permute-start.52 = (bf16[128,3072]{1,0:T(8,128)(2,1)S(1)}, bf16[128,3072]{1,0:T(8,128)(2,1)S(1)}, u32[]{:S(2)}, u32[]{:S(2)}) collective-permute-start(bf16[128,3072]{1,0:T(8,128)(2,1)S(1)} %get-tuple-element.215), channel_id=1, source_target_pairs={{0,4},{4,0},{1,5},{5,1},{2,6},{6,2},{3,7},{7,3},{8,12},{12,8},{9,1... | collective-permute-start | bytes 2359304 | tf_op jit(solution)/shard_map/ppermute | solution.py:234
  582.8 20.9 %collective-permute-start.54 = (bf16[512,1024]{1,0:T(8,128)(2,1)S(1)}, bf16[512,1024]{1,0:T(8,128)(2,1)S(1)}, u32[]{:S(2)}, u32[]{:S(2)}) collective-permute-start(bf16[512,1024]{1,0:T(8,128)(2,1)S(1)} %get-tuple-element.251), channel_id=1, source_target_pairs={{0,1},{1,0},{2,3},{3,2},{4,5},{5,4},{6,7},{7,6},{8,9},{9,8},{10,11... | collective-permute-start | bytes 3145736 | tf_op jit(solution)/shard_map/ppermute | solution.py:234
  (95 other events, 1300.3 us)

commit v3 on v2

--- a/solution.py
+++ b/solution.py
@@ -252,19 +252,19 @@
 
 
 class Chain:
-    def __init__(self, steps):
-        self.steps, self.value = steps, None
+    def __init__(self, steps, ties=1):
+        self.steps, self.value, self.ties = steps, None, ties
         self.waiting = next(steps)
 
     def go(self, *beside):
-        ready = self.waiting
-        if beside:
-            tied = lax.optimization_barrier((beside, ready))
-            beside, ready = tied
-        try:
-            self.waiting = self.steps.send(ready)
-        except StopIteration as stop:
-            self.value = stop.value
+        for _ in range(self.ties):
+            ready = self.waiting
+            if beside:
+                beside, ready = lax.optimization_barrier((beside, ready))
+            try:
+                self.waiting = self.steps.send(ready)
+            except StopIteration as stop:
+                self.value = stop.value
         return beside[0] if len(beside) == 1 else beside
 
 
@@ -366,22 +366,21 @@
 def scatter_steps(keep, send):
     width = keep.shape[1]
     (send,) = yield (send,)
-    came = swap(send, "c")
+    (send,) = yield (send,)
+    (came,) = yield (swap(send, "c"),)
 
     def part(i):
         rows = slice(i * 128, (i + 1) * 128)
         return plus(keep[rows], came[rows])
 
     a_send, b_send = yield (part(1), part(3))
-    a_got = swap(a_send, "y")
-    b_got = swap(b_send, "x")
+    a_got, b_got = yield (swap(a_send, "y"), swap(b_send, "x"))
     a_keep, b_keep = part(0), part(2)
     a_next, b_next = yield (
         plus(a_keep[64:], a_got[64:]),
         plus(b_keep[64:], b_got[64:]),
     )
-    a_last = swap(a_next, "x")
-    b_last = swap(b_next, "y")
+    a_last, b_last = yield (swap(a_next, "x"), swap(b_next, "y"))
     a_half = plus(a_keep[:64], a_got[:64])
     b_half = plus(b_keep[:64], b_got[:64])
 
@@ -396,7 +395,7 @@
         )
 
     (low,) = yield (both(1),)
-    low_got = swap(low, "zl")
+    (low_got,) = yield (swap(low, "zl"),)
     kept = both(0)
     (high,) = yield (plus(kept[1], low_got[1]),)
     total = kept[0].astype(F32) + low_got[0].astype(F32) + swap(high, "zh").astype(F32)
@@ -682,7 +681,7 @@
     residual = inputs_f + nn(attended, full_out)
     normed_two, inverse_two = standardize(residual)
     second = (normed_two * full_two).astype(BF)
-    second = three.go(second)
+    second, full_gate, full_up = three.go(second, full_gate, full_up)
     full_down = assemble(three.value, coords, padded, 896, 0)
     hidden, d_gate, d_up = feed_call(second, grad_low, full_gate, full_up, full_down)
 
@@ -693,12 +692,12 @@
     def grad_of(left, right, start, total, carry):
         return grad_call(coords, left, right, col_spec, padded, block, total, start, carry)
 
-    down = Chain(scatter_steps(*grad_of(grad_low, hidden, 0, padded, None)))
+    down = Chain(scatter_steps(*grad_of(grad_low, hidden, 0, padded, None)), 2)
     d_gate = down.go(d_gate)
     sums = grad_of(second, d_gate, 0, 2 * padded, None)
     sums, d_up = down.go(sums, d_up)
     sums = grad_of(second, d_up, per, 2 * padded, sums)
-    feed = Chain(scatter_steps(*sums))
+    feed = Chain(scatter_steps(*sums), 2)
     d_gate = feed.go(d_gate)
     d_gate = down.go(d_gate)
     grad_second = nt(d_gate, full_gate)
@@ -711,7 +710,8 @@
     datt = nt(grad_proj, full_out).astype(BF)
     out_spec = pl.BlockSpec((1024, 512), lambda j: (0, j))
     out = Chain(
-        scatter_steps(*grad_call(coords, attended, grad_proj, out_spec, 1024, 512, 1024, 0, None))
+        scatter_steps(*grad_call(coords, attended, grad_proj, out_spec, 1024, 512, 1024, 0, None)),
+        2,
     )
     datt = out.go(datt)
     datt = down.go(datt)
@@ -732,7 +732,8 @@
 
     qkv_spec = pl.BlockSpec((1, 1024, 1024), lambda j: (j, 0, 0))
     last = Chain(
-        scatter_steps(*grad_call(coords, first, fused, qkv_spec, 3072, 1024, 3072, 0, None))
+        scatter_steps(*grad_call(coords, first, fused, qkv_spec, 3072, 1024, 3072, 0, None)),
+        2,
     )
     fused = last.go(fused)
     grad_first = nt(fused[0], full_qkv[:, :1024])

time: 610 us -> 597 us (0.979)
  waiting for transfers between devices: 166 us -> 140 us
    ppermute x67, waiting for transfers between devices: 166 us -> 140 us  [swap(): return lax.ppermute(values, axis, [(0, 1), (1, 0)])]
  transfers between devices with their start and end apart: 67 -> 67, of which waited for: 28 -> 28; matrix products, arithmetic and copies ran while one was open for 16% -> 19% of each run, Pallas kernels for 28% -> 28%
where the time goes in v3:
time: 597 us; the launch traced here: 592 us
  Pallas kernels  245 us (41%)
  waiting for transfers between devices  140 us (23%)
  starting transfers between devices  66.7 us (11%)
  other arithmetic  66.6 us (11%)
  matrix products  53 us (9%)
  local copies, waits for them, and re-layouts  18.6 us (3%)
    ppermute x67, waiting for transfers between devices, swap(): return lax.ppermute(values, axis, [(0, 1), (1, 0)])  140 us
    pallas_call x4, Pallas kernels, attend_back_call(): pl.pallas_call(attend_back_kernel, grid=(count,), out_shape=jax.ShapeDtyp...  67.4 us
    ppermute x67, starting transfers between devices, swap(): return lax.ppermute(values, axis, [(0, 1), (1, 0)])  66.7 us
    pallas_call x5, Pallas kernels, grad_call(): pl.pallas_call(grad_kernel, grid=(steps,), out_shape=[jax.ShapeDtypeStruc...  54.3 us
    dot_general x7, matrix products, nt(): lax.dot_general(left, right, (((1,), (1,)), ((), ())), preferred_element_...  48.4 us
    pallas_call x3, Pallas kernels, attend_call(): pl.pallas_call(attend_kernel, grid=(count,), out_shape=[jax.ShapeDtypeStr...  43.1 us
    pallas_call x6, Pallas kernels, assemble(): pl.pallas_call(assemble_kernel, grid=(width // block,), out_shape=jax.Sha...  31 us
    pallas_call x1, Pallas kernels, feed_call(): pl.pallas_call(feed_kernel, grid=(width // block,), out_shape=[jax.ShapeD...  29.4 us
  transfers between devices with their start and end apart: 67, of which 28 were waited for; matrix products, arithmetic and copies ran while one was open for 19% of the time, Pallas kernels for 28%

profile of v3, /device:TPU:0, one launch (start us, length us, event | category | flops | bytes accessed | tf_op | source)
XLA Modules:
  0.0 591.9 jit_solution(18306900619953597143)
XLA Ops:
  17.8 9.0 %collective-permute-done.2 = bf16[2,2,16,3200]{3,2,0,1:T(8,128)(2,1)S(1)} collective-permute-done((bf16[2,2,16,3200]{3,2,0,1:T(8,128)(2,1)S(1)}, bf16[2,2,16,3200]{3,2,0,1:T(8,128)(2,1)S(1)}, u32[]{:S(2)}, u32[]{:S(2)}) %collective-permute-start.2) | collective-permute-done | bytes 409632 | tf_op jit(solution)/shard_map/ppermute | solution.py:234
  64.5 14.8 %collective-permute-done.12 = bf16[2,2,16,6400]{3,2,0,1:T(8,128)(2,1)S(1)} collective-permute-done((bf16[2,2,16,6400]{3,2,0,1:T(8,128)(2,1)S(1)}, bf16[2,2,16,6400]{3,2,0,1:T(8,128)(2,1)S(1)}, u32[]{:S(2)}, u32[]{:S(2)}) %collective-permute-start.12) | collective-permute-done | bytes 819232 | tf_op jit(solution)/shard_map/ppermute | solution.py:234
  81.7 6.6 %assemble.7.w_ref = bf16[1024,3072]{1,0:T(8,128)(2,1)} custom-call(s32[5]{0:T(128)} %stack.111.coords, bf16[8,16,3200]{2,1,0:T(8,128)(2,1)} %copy-done.14, bf16[8,16,3200]{2,1,0:T(8,128)(2,1)} %copy-done.20, bf16[8,16,3200]{2,1,0:T(8,128)(2,1)} %copy-done.13, bf16[8,16,3200]{2,1,0:T(8,128)(2,1)} %copy-done.19, bf16[8,16,3200]{2,1,0:T(8,128)(2,1)} %copy-done.23, ...), custom_call_target="tpu_custom_call" | custom-call | flops 2800000000 | bytes 4000000 | tf_op jit(solution)/shard_map/assemble/pallas_call | solution.py:308
  95.1 19.7 %norm_qkv.1 = (bf16[1024,1024]{1,0:T(8,128)(2,1)}, bf16[1024,3072]{1,0:T(8,128)(2,1)}) custom-call(bf16[1024,1024]{1,0:T(8,128)(2,1)} %get-tuple-element.312.tok_ref, f32[1,1024]{1,0:T(1,128)} %get-tuple-element.386.gain_ref, bf16[1024,3072]{1,0:T(8,128)(2,1)} %assemble.7.w_ref, f32[1024,128]{1,0:T(8,128)} %get-tuple-element.396.cos_ref, ...), custom_call_target="tpu_custom_call" | custom-call | flops 14000000000 | bytes 20000000 | tf_op jit(solution)/shard_map/norm_qkv/pallas_call | solution.py:442
  120.5 15.9 %attend.3 = (bf16[1024,1024]{1,0:T(8,128)(2,1)}, f32[1024,1024]{1,0:T(8,128)}) custom-call(bf16[1024,3072]{1,0:T(8,128)(2,1)} %get-tuple-element.171.q_ref.k_ref.v_ref, bf16[1024,3072]{1,0:T(8,128)(2,1)} %get-tuple-element.171.q_ref.k_ref.v_ref, bf16[1024,3072]{1,0:T(8,128)(2,1)} %get-tuple-element.171.q_ref.k_ref.v_ref), custom_call_target="tpu_custom_call" | custom-call | flops 10499999744 | bytes 15000000 | tf_op jit(solution)/shard_map/attend/pallas_call | solution.py:496
  140.7 20.5 %attend.4 = (bf16[1024,1024]{1,0:T(8,128)(2,1)}, f32[1024,1024]{1,0:T(8,128)}) custom-call(bf16[1024,3072]{1,0:T(8,128)(2,1)} %get-tuple-element.171.q_ref.k_ref.v_ref, bf16[1024,3072]{1,0:T(8,128)(2,1)} %get-tuple-element.171.q_ref.k_ref.v_ref, ...), custom_call_target="tpu_custom_call", output_to_operand_aliasing={{0}: (3, {}), {1}: (4, {})} | custom-call | flops 14000000000 | bytes 20000000 | tf_op jit(solution)/shard_map/attend/pallas_call | solution.py:496
  161.2 15.9 %collective-permute-done.18 = bf16[4,16,2688]{2,1,0:T(8,128)(2,1)S(1)} collective-permute-done((bf16[4,16,2688]{2,1,0:T(8,128)(2,1)S(1)}, bf16[4,16,2688]{2,1,0:T(8,128)(2,1)S(1)}, u32[]{:S(2)}, u32[]{:S(2)}) %collective-permute-start.18) | collective-permute-done | bytes 344096 | tf_op jit(solution)/shard_map/ppermute | solution.py:234
  179.0 6.7 %attend.5 = (bf16[1024,1024]{1,0:T(8,128)(2,1)}, f32[1024,1024]{1,0:T(8,128)}) custom-call(bf16[1024,3072]{1,0:T(8,128)(2,1)} %get-tuple-element.171.q_ref.k_ref.v_ref, bf16[1024,3072]{1,0:T(8,128)(2,1)} %get-tuple-element.171.q_ref.k_ref.v_ref, ...), custom_call_target="tpu_custom_call", output_to_operand_aliasing={{0}: (3, {}), {1}: (4, {})} | custom-call | flops 3500000000 | bytes 5000000 | tf_op jit(solution)/shard_map/attend/pallas_call | solution.py:496
  240.6 29.4 %feed.1 = (bf16[1024,2688]{1,0:T(8,128)(2,1)}, bf16[1024,2688]{1,0:T(8,128)(2,1)}, bf16[1024,2688]{1,0:T(8,128)(2,1)}) custom-call(bf16[1024,1024]{1,0:T(8,128)(2,1)} %multiply_convert_fusion.second_ref.x_ref, bf16[1024,1024]{1,0:T(8,128)(2,1)} %maximum_select_fusion.1.grad_ref.x_ref, bf16[1024,2688]{1,0:T(8,128)(2,1)} %assemble.9.gate_ref, ...), custom_call_target="tpu_custom_call" | custom-call | flops 20999999488 | bytes 30000000 | tf_op jit(solution)/shard_map/feed/pallas_call | solution.py:604
  269.9 11.8 %weight_grad.5 = (bf16[512,2688]{1,0:T(8,128)(2,1)}, bf16[512,2688]{1,0:T(8,128)(2,1)}) custom-call(s32[5]{0:T(128)} %stack.111.coords, bf16[1024,1024]{1,0:T(8,128)(2,1)} %maximum_select_fusion.1.grad_ref.x_ref, bf16[1024,2688]{1,0:T(8,128)(2,1)} %get-tuple-element.203.y_ref), custom_call_target="tpu_custom_call" | custom-call | flops 8180869632 | bytes 11686956 | tf_op jit(solution)/shard_map/weight_grad/pallas_call | solution.py:349
  283.1 11.8 %weight_grad.6 = (bf16[512,5376]{1,0:T(8,128)(2,1)}, bf16[512,5376]{1,0:T(8,128)(2,1)}) custom-call(s32[5]{0:T(128)} %stack.111.coords, bf16[1024,1024]{1,0:T(8,128)(2,1)} %multiply_convert_fusion.second_ref.x_ref, bf16[1024,2688]{1,0:T(8,128)(2,1)} %get-tuple-element.225.y_ref), custom_call_target="tpu_custom_call" | custom-call | flops 8180869632 | bytes 11686956 | tf_op jit(solution)/shard_map/weight_grad/pallas_call | solution.py:349
  298.4 12.0 %weight_grad.7 = (bf16[512,5376]{1,0:T(8,128)(2,1)}, bf16[512,5376]{1,0:T(8,128)(2,1)}) custom-call(s32[5]{0:T(128)} %stack.111.coords, bf16[1024,1024]{1,0:T(8,128)(2,1)} %multiply_convert_fusion.second_ref.x_ref, bf16[1024,2688]{1,0:T(8,128)(2,1)} %get-tuple-element.232.y_ref, ...), custom_call_target="tpu_custom_call", output_to_operand_aliasing={{0}: (3, {}), {1}: (4, {})} | custom-call | flops 8180869632 | bytes 11686956 | tf_op jit(solution)/shard_map/weight_grad/pallas_call | solution.py:349
  311.8 11.5 %add_convert_fusion = bf16[1024,1024]{1,0:T(8,128)(2,1)} fusion(f32[1024,1024]{1,0:T(8,128)} %copy-done, bf16[1024,2688]{1,0:T(8,128)(2,1)} %get-tuple-element.203.y_ref, bf16[1024,2688]{1,0:T(8,128)(2,1)} %assemble.11.down_ref), kind=kOutput, calls=%fused_computation.17 | convolution fusion | flops 5639241728 | bytes 17301504 | tf_op jit(solution)/shard_map/dot_general | solution.py:238
  332.8 9.4 %fusion.64 = f32[1024,1024]{1,0:T(8,128)} fusion(bf16[1024,2688]{1,0:T(8,128)(2,1)} %get-tuple-element.225.y_ref, bf16[1024,2688]{1,0:T(8,128)(2,1)S(1)} %bitcast.184), kind=kOutput, calls=%fused_computation.219 | convolution fusion | flops 5637144576 | bytes 15204352 | tf_op jit(solution)/shard_map/dot_general | solution.py:238
  345.5 10.0 %multiply_reduce_fusion = (f32[1024]{0:T(1024)S(1)}, f32[1024]{0:T(1024)S(1)}, f32[1024]{0:T(1024)S(1)}, f32[1024,1024]{1,0:T(8,128)S(1)}) fusion(f32[1024,1024]{1,0:T(8,128)S(1)} %copy-done.1, f32[1024]{0:T(1024)S(1)} %add_rsqrt_fusion.1, f32[1024]{0:T(1024)S(1)} %broadcast_multiply_fusion.5, f32[1024]{0:T(1024)S(1)} %bitcast.234, ...), kind=kOutput, calls=%fused_computation.15 | convolution fusion | flops 5646578688 | bytes 23617536 | tf_op jit(solution)/shard_map/dot_general | solution.py:238
  378.1 16.8 %attend_back.4.refs_0_ = bf16[3,1024,1024]{2,1,0:T(8,128)(2,1)} custom-call(bf16[1024,3072]{1,0:T(8,128)(2,1)} %get-tuple-element.171.q_ref.k_ref.v_ref, bf16[1024,3072]{1,0:T(8,128)(2,1)} %get-tuple-element.171.q_ref.k_ref.v_ref, bf16[1024,3072]{1,0:T(8,128)(2,1)} %get-tuple-element.171.q_ref.k_ref.v_ref, ...), custom_call_target="tpu_custom_call" | custom-call | flops 10499999744 | bytes 15000000 | tf_op jit(solution)/shard_map/attend_back/pallas_call | solution.py:564
  396.7 7.4 %collective-permute-done.39 = bf16[128,5376]{1,0:T(8,128)(2,1)} collective-permute-done((bf16[128,5376]{1,0:T(8,128)(2,1)}, bf16[128,5376]{1,0:T(8,128)(2,1)}, u32[]{:S(2)}, u32[]{:S(2)}) %collective-permute-start.39) | collective-permute-done | bytes 1376288 | tf_op jit(solution)/shard_map/ppermute | solution.py:234
  416.1 16.8 %attend_back.5.refs_0_ = bf16[3,1024,1024]{2,1,0:T(8,128)(2,1)} custom-call(bf16[1024,3072]{1,0:T(8,128)(2,1)} %get-tuple-element.171.q_ref.k_ref.v_ref, bf16[1024,3072]{1,0:T(8,128)(2,1)} %get-tuple-element.171.q_ref.k_ref.v_ref, bf16[1024,3072]{1,0:T(8,128)(2,1)} %get-tuple-element.171.q_ref.k_ref.v_ref, ...), custom_call_target="tpu_custom_call", output_to_operand_aliasing={{}: (8, {})} | custom-call | flops 10499999744 | bytes 15000000 | tf_op jit(solution)/shard_map/attend_back/pallas_call | solution.py:564
  440.8 17.0 %attend_back.6.refs_0_ = bf16[3,1024,1024]{2,1,0:T(8,128)(2,1)} custom-call(bf16[1024,3072]{1,0:T(8,128)(2,1)} %get-tuple-element.171.q_ref.k_ref.v_ref, bf16[1024,3072]{1,0:T(8,128)(2,1)} %get-tuple-element.171.q_ref.k_ref.v_ref, bf16[1024,3072]{1,0:T(8,128)(2,1)} %get-tuple-element.171.q_ref.k_ref.v_ref, ...), custom_call_target="tpu_custom_call", output_to_operand_aliasing={{}: (8, {})} | custom-call | flops 10499999744 | bytes 15000000 | tf_op jit(solution)/shard_map/attend_back/pallas_call | solution.py:564
  459.4 16.8 %attend_back.7.y_ref = bf16[3,1024,1024]{2,1,0:T(8,128)(2,1)} custom-call(bf16[1024,3072]{1,0:T(8,128)(2,1)} %get-tuple-element.171.q_ref.k_ref.v_ref, bf16[1024,3072]{1,0:T(8,128)(2,1)} %get-tuple-element.171.q_ref.k_ref.v_ref, bf16[1024,3072]{1,0:T(8,128)(2,1)} %get-tuple-element.171.q_ref.k_ref.v_ref, ...), custom_call_target="tpu_custom_call", output_to_operand_aliasing={{}: (8, {})} | custom-call | flops 10499999744 | bytes 15000000 | tf_op jit(solution)/shard_map/attend_back/pallas_call | solution.py:564
  476.3 12.2 %weight_grad.9 = (bf16[512,3072]{1,0:T(8,128)(2,1)}, bf16[512,3072]{1,0:T(8,128)(2,1)}) custom-call(s32[5]{0:T(128)} %stack.111.coords, bf16[1024,1024]{1,0:T(8,128)(2,1)} %get-tuple-element.284.x_ref, bf16[3,1024,1024]{2,1,0:T(8,128)(2,1)} %attend_back.7.y_ref), custom_call_target="tpu_custom_call" | custom-call | flops 9349565440 | bytes 13356521 | tf_op jit(solution)/shard_map/weight_grad/pallas_call | solution.py:349
  500.6 13.7 %collective-permute-done.59 = bf16[2,16,1024]{2,1,0:T(8,128)(2,1)S(1)} collective-permute-done((bf16[2,16,1024]{2,1,0:T(8,128)(2,1)S(1)}, bf16[2,16,1024]{2,1,0:T(8,128)(2,1)S(1)}, u32[]{:S(2)}, u32[]{:S(2)}) %collective-permute-start.59) | collective-permute-done | bytes 65568 | tf_op jit(solution)/shard_map/ppermute | solution.py:234
  529.3 12.2 %collective-permute-done.52 = bf16[128,3072]{1,0:T(8,128)(2,1)S(1)} collective-permute-done((bf16[128,3072]{1,0:T(8,128)(2,1)S(1)}, bf16[128,3072]{1,0:T(8,128)(2,1)S(1)}, u32[]{:S(2)}, u32[]{:S(2)}) %collective-permute-start.52) | collective-permute-done | bytes 786464 | tf_op jit(solution)/shard_map/ppermute | solution.py:234
  572.5 11.0 %collective-permute-done.58 = bf16[2,16,3072]{2,1,0:T(8,128)(2,1)S(1)} collective-permute-done((bf16[2,16,3072]{2,1,0:T(8,128)(2,1)S(1)}, bf16[2,16,3072]{2,1,0:T(8,128)(2,1)S(1)}, u32[]{:S(2)}, u32[]{:S(2)}) %collective-permute-start.58) | collective-permute-done | bytes 196640 | tf_op jit(solution)/shard_map/ppermute | solution.py:234
  (343 shorter events, 260.8 us)
Async XLA Ops:
  9.3 42.5 %collective-permute-start = (bf16[512,1024]{1,0:T(8,128)(2,1)}, bf16[512,1024]{1,0:T(8,128)(2,1)}, u32[]{:S(2)}, u32[]{:S(2)}) collective-permute-start(bf16[512,1024]{1,0:T(8,128)(2,1)} %get-tuple-element.341), channel_id=1, source_target_pairs={{0,1},{1,0},{2,3},{3,2},{4,5},{5,4},{6,7},{7,6},{8,9},{9,8},{10,11... | collective-permute-start | bytes 3145736 | tf_op jit(solution)/shard_map/ppermute | solution.py:234
  29.8 20.9 %collective-permute-start.3 = (bf16[2,16,6400]{2,1,0:T(8,128)(2,1)}, bf16[2,16,6400]{2,1,0:T(8,128)(2,1)S(1)}, u32[]{:S(2)}, u32[]{:S(2)}) collective-permute-start(bf16[2,16,6400]{2,1,0:T(8,128)(2,1)} %bitcast.17), channel_id=1, source_target_pairs={{0,16},{16,0},{1,17},{17,1},{2,18},{18,2},{3,19},{19,3},{4,20},{20... | collective-permute-start | bytes 1228808 | tf_op jit(solution)/shard_map/ppermute | solution.py:234
  37.0 23.5 %collective-permute-start.7 = (bf16[8,16,3200]{2,1,0:T(8,128)(2,1)S(1)}, bf16[8,16,3200]{2,1,0:T(8,128)(2,1)S(1)}, u32[]{:S(2)}, u32[]{:S(2)}) collective-permute-start(bf16[8,16,3200]{2,1,0:T(8,128)(2,1)S(1)} %constant_dynamic-update-slice_fusion.2.refs_2_), channel_id=1, source_target_pairs={{0,1},{1,0},{2,3},{3,2},{4,5},{5,4},{6,7},{7,6},{8,9},{9,8},{10,11... | collective-permute-start | bytes 2457608 | tf_op jit(solution)/shard_map/ppermute | solution.py:234
  88.3 26.6 %collective-permute-start.15 = (bf16[2,16,2688]{2,1,0:T(8,128)(2,1)S(1)}, bf16[2,16,2688]{2,1,0:T(8,128)(2,1)S(1)}, u32[]{:S(2)}, u32[]{:S(2)}) collective-permute-start(bf16[2,16,2688]{2,1,0:T(8,128)(2,1)S(1)} %bitcast.210), channel_id=1, source_target_pairs={{0,16},{16,0},{1,17},{17,1},{2,18},{18,2},{3,19},{19,3},{4,20},{20... | collective-permute-start | bytes 516104 | tf_op jit(solution)/shard_map/ppermute | solution.py:234
  89.3 25.6 %collective-permute-start.14 = (bf16[4,16,6400]{2,1,0:T(8,128)(2,1)S(1)}, bf16[4,16,6400]{2,1,0:T(8,128)(2,1)}, u32[]{:S(2)}, u32[]{:S(2)}) collective-permute-start(bf16[4,16,6400]{2,1,0:T(8,128)(2,1)S(1)} %pad_maximum_fusion.4), channel_id=1, source_target_pairs={{0,4},{4,0},{1,5},{5,1},{2,6},{6,2},{3,7},{7,3},{8,12},{12,8},{9,1... | collective-permute-start | bytes 2457608 | tf_op jit(solution)/shard_map/ppermute | solution.py:234
  90.1 27.3 %collective-permute-start.13 = (bf16[4,16,6400]{2,1,0:T(8,128)(2,1)S(1)}, bf16[4,16,6400]{2,1,0:T(8,128)(2,1)S(1)}, u32[]{:S(2)}, u32[]{:S(2)}) collective-permute-start(bf16[4,16,6400]{2,1,0:T(8,128)(2,1)S(1)} %pad_maximum_fusion.3), channel_id=1, source_target_pairs={{0,1},{1,0},{2,3},{3,2},{4,5},{5,4},{6,7},{7,6},{8,9},{9,8},{10,11... | collective-permute-start | bytes 2457608 | tf_op jit(solution)/shard_map/ppermute | solution.py:234
  136.4 49.4 %collective-permute-start.19 = (bf16[8,16,6400]{2,1,0:T(8,128)(2,1)}, bf16[8,16,6400]{2,1,0:T(8,128)(2,1)}, u32[]{:S(2)}, u32[]{:S(2)}) collective-permute-start(bf16[8,16,6400]{2,1,0:T(8,128)(2,1)} %pad_maximum_fusion.refs_0_), channel_id=1, source_target_pairs={{0,4},{4,0},{1,5},{5,1},{2,6},{6,2},{3,7},{7,3},{8,12},{12,8},{9,1... | collective-permute-start | bytes 4915208 | tf_op jit(solution)/shard_map/ppermute | solution.py:234
  137.0 48.8 %collective-permute-start.20 = (bf16[8,16,6400]{2,1,0:T(8,128)(2,1)}, bf16[8,16,6400]{2,1,0:T(8,128)(2,1)}, u32[]{:S(2)}, u32[]{:S(2)}) collective-permute-start(bf16[8,16,6400]{2,1,0:T(8,128)(2,1)} %pad_maximum_fusion.1.refs_2_), channel_id=1, source_target_pairs={{0,1},{1,0},{2,3},{3,2},{4,5},{5,4},{6,7},{7,6},{8,9},{9,8},{10,11... | collective-permute-start | bytes 4915208 | tf_op jit(solution)/shard_map/ppermute | solution.py:234
  137.7 39.4 %collective-permute-start.18 = (bf16[4,16,2688]{2,1,0:T(8,128)(2,1)S(1)}, bf16[4,16,2688]{2,1,0:T(8,128)(2,1)S(1)}, u32[]{:S(2)}, u32[]{:S(2)}) collective-permute-start(bf16[4,16,2688]{2,1,0:T(8,128)(2,1)S(1)} %pad_maximum_fusion.17), channel_id=1, source_target_pairs={{0,4},{4,0},{1,5},{5,1},{2,6},{6,2},{3,7},{7,3},{8,12},{12,8},{9,1... | collective-permute-start | bytes 1032200 | tf_op jit(solution)/shard_map/ppermute | solution.py:234
  139.2 38.8 %collective-permute-start.17 = (bf16[4,16,2688]{2,1,0:T(8,128)(2,1)S(1)}, bf16[4,16,2688]{2,1,0:T(8,128)(2,1)S(1)}, u32[]{:S(2)}, u32[]{:S(2)}) collective-permute-start(bf16[4,16,2688]{2,1,0:T(8,128)(2,1)S(1)} %pad_maximum_fusion.16), channel_id=1, source_target_pairs={{0,1},{1,0},{2,3},{3,2},{4,5},{5,4},{6,7},{7,6},{8,9},{9,8},{10,11... | collective-permute-start | bytes 1032200 | tf_op jit(solution)/shard_map/ppermute | solution.py:234
  188.0 41.2 %collective-permute-start.27 = (bf16[512,1024]{1,0:T(8,128)(2,1)}, bf16[512,1024]{1,0:T(8,128)(2,1)}, u32[]{:S(2)}, u32[]{:S(2)}) collective-permute-start(bf16[512,1024]{1,0:T(8,128)(2,1)} %get-tuple-element.340), channel_id=1, source_target_pairs={{0,1},{1,0},{2,3},{3,2},{4,5},{5,4},{6,7},{7,6},{8,9},{9,8},{10,11... | collective-permute-start | bytes 3145736 | tf_op jit(solution)/shard_map/ppermute | solution.py:234
  189.7 34.9 %collective-permute-start.25 = (bf16[8,16,2688]{2,1,0:T(8,128)(2,1)}, bf16[8,16,2688]{2,1,0:T(8,128)(2,1)}, u32[]{:S(2)}, u32[]{:S(2)}) collective-permute-start(bf16[8,16,2688]{2,1,0:T(8,128)(2,1)} %pad_maximum_fusion.5.refs_0_), channel_id=1, source_target_pairs={{0,4},{4,0},{1,5},{5,1},{2,6},{6,2},{3,7},{7,3},{8,12},{12,8},{9,1... | collective-permute-start | bytes 2064392 | tf_op jit(solution)/shard_map/ppermute | solution.py:234
  192.0 36.2 %collective-permute-start.26 = (bf16[8,16,2688]{2,1,0:T(8,128)(2,1)}, bf16[8,16,2688]{2,1,0:T(8,128)(2,1)}, u32[]{:S(2)}, u32[]{:S(2)}) collective-permute-start(bf16[8,16,2688]{2,1,0:T(8,128)(2,1)} %pad_maximum_fusion.6.refs_2_), channel_id=1, source_target_pairs={{0,1},{1,0},{2,3},{3,2},{4,5},{5,4},{6,7},{7,6},{8,9},{9,8},{10,11... | collective-permute-start | bytes 2064392 | tf_op jit(solution)/shard_map/ppermute | solution.py:234
  311.8 30.4 %collective-permute-start.35 = (bf16[512,5376]{1,0:T(8,128)(2,1)}, bf16[512,5376]{1,0:T(8,128)(2,1)S(1)}, u32[]{:S(2)}, u32[]{:S(2)}) collective-permute-start(bf16[512,5376]{1,0:T(8,128)(2,1)} %get-tuple-element.226), channel_id=1, source_target_pairs={{0,2},{2,0},{1,3},{3,1},{4,6},{6,4},{5,7},{7,5},{8,10},{10,8},{9,1... | collective-permute-start | bytes 16515080 | tf_op jit(solution)/shard_map/ppermute | solution.py:234
  331.1 27.8 %collective-permute-start.36 = (bf16[64,2688]{1,0:T(8,128)(2,1)}, bf16[64,2688]{1,0:T(8,128)(2,1)S(1)}, u32[]{:S(2)}, u32[]{:S(2)}) collective-permute-start(bf16[64,2688]{1,0:T(8,128)(2,1)} %get-tuple-element.233), channel_id=1, source_target_pairs={{0,1},{1,0},{2,3},{3,2},{4,5},{5,4},{6,7},{7,6},{8,9},{9,8},{10,11... | collective-permute-start | bytes 1032200 | tf_op jit(solution)/shard_map/ppermute | solution.py:234
  331.6 27.3 %collective-permute-start.37 = (bf16[64,2688]{1,0:T(8,128)(2,1)}, bf16[64,2688]{1,0:T(8,128)(2,1)S(1)}, u32[]{:S(2)}, u32[]{:S(2)}) collective-permute-start(bf16[64,2688]{1,0:T(8,128)(2,1)} %get-tuple-element.234), channel_id=1, source_target_pairs={{0,4},{4,0},{1,5},{5,1},{2,6},{6,2},{3,7},{7,3},{8,12},{12,8},{9,1... | collective-permute-start | bytes 1032200 | tf_op jit(solution)/shard_map/ppermute | solution.py:234
  372.6 31.4 %collective-permute-start.39 = (bf16[128,5376]{1,0:T(8,128)(2,1)}, bf16[128,5376]{1,0:T(8,128)(2,1)}, u32[]{:S(2)}, u32[]{:S(2)}) collective-permute-start(bf16[128,5376]{1,0:T(8,128)(2,1)} %get-tuple-element.245), channel_id=1, source_target_pairs={{0,4},{4,0},{1,5},{5,1},{2,6},{6,2},{3,7},{7,3},{8,12},{12,8},{9,1... | collective-permute-start | bytes 4128776 | tf_op jit(solution)/shard_map/ppermute | solution.py:234
  373.6 31.0 %collective-permute-start.40 = (bf16[128,5376]{1,0:T(8,128)(2,1)}, bf16[128,5376]{1,0:T(8,128)(2,1)}, u32[]{:S(2)}, u32[]{:S(2)}) collective-permute-start(bf16[128,5376]{1,0:T(8,128)(2,1)} %get-tuple-element.246), channel_id=1, source_target_pairs={{0,1},{1,0},{2,3},{3,2},{4,5},{5,4},{6,7},{7,6},{8,9},{9,8},{10,11... | collective-permute-start | bytes 4128776 | tf_op jit(solution)/shard_map/ppermute | solution.py:234
  375.0 34.7 %collective-permute-start.41 = (bf16[512,1024]{1,0:T(8,128)(2,1)}, bf16[512,1024]{1,0:T(8,128)(2,1)}, u32[]{:S(2)}, u32[]{:S(2)}) collective-permute-start(bf16[512,1024]{1,0:T(8,128)(2,1)} %get-tuple-element.251), channel_id=1, source_target_pairs={{0,2},{2,0},{1,3},{3,1},{4,6},{6,4},{5,7},{7,5},{8,10},{10,8},{9,1... | collective-permute-start | bytes 3145736 | tf_op jit(solution)/shard_map/ppermute | solution.py:234
  413.9 21.4 %collective-permute-start.44 = (bf16[128,1024]{1,0:T(8,128)(2,1)}, bf16[128,1024]{1,0:T(8,128)(2,1)}, u32[]{:S(2)}, u32[]{:S(2)}) collective-permute-start(bf16[128,1024]{1,0:T(8,128)(2,1)} %get-tuple-element.262), channel_id=1, source_target_pairs={{0,4},{4,0},{1,5},{5,1},{2,6},{6,2},{3,7},{7,3},{8,12},{12,8},{9,1... | collective-permute-start | bytes 786440 | tf_op jit(solution)/shard_map/ppermute | solution.py:234
  488.5 27.5 %collective-permute-start.51 = (bf16[512,3072]{1,0:T(8,128)(2,1)}, bf16[512,3072]{1,0:T(8,128)(2,1)S(1)}, u32[]{:S(2)}, u32[]{:S(2)}) collective-permute-start(bf16[512,3072]{1,0:T(8,128)(2,1)} %get-tuple-element.287), channel_id=1, source_target_pairs={{0,2},{2,0},{1,3},{3,1},{4,6},{6,4},{5,7},{7,5},{8,10},{10,8},{9,1... | collective-permute-start | bytes 9437192 | tf_op jit(solution)/shard_map/ppermute | solution.py:234
  491.6 53.3 %collective-permute-start.46 = (bf16[512,1024]{1,0:T(8,128)(2,1)S(1)}, bf16[512,1024]{1,0:T(8,128)(2,1)S(1)}, u32[]{:S(2)}, u32[]{:S(2)}) collective-permute-start(bf16[512,1024]{1,0:T(8,128)(2,1)S(1)} %get-tuple-element.334), channel_id=1, source_target_pairs={{0,1},{1,0},{2,3},{3,2},{4,5},{5,4},{6,7},{7,6},{8,9},{9,8},{10,11... | collective-permute-start | bytes 3145736 | tf_op jit(solution)/shard_map/ppermute | solution.py:234
  493.0 21.9 %collective-permute-start.60 = (bf16[2,16,5376]{2,1,0:T(8,128)(2,1)S(1)}, bf16[2,16,5376]{2,1,0:T(8,128)(2,1)S(1)}, u32[]{:S(2)}, u32[]{:S(2)}) collective-permute-start(bf16[2,16,5376]{2,1,0:T(8,128)(2,1)S(1)} %copy-done.30), channel_id=1, source_target_pairs={{0,16},{16,0},{1,17},{17,1},{2,18},{18,2},{3,19},{19,3},{4,20},{20... | collective-permute-start | bytes 1032200 | tf_op jit(solution)/shard_map/ppermute | solution.py:234
  564.9 25.1 %collective-permute-start.54 = (bf16[512,1024]{1,0:T(8,128)(2,1)S(1)}, bf16[512,1024]{1,0:T(8,128)(2,1)S(1)}, u32[]{:S(2)}, u32[]{:S(2)}) collective-permute-start(bf16[512,1024]{1,0:T(8,128)(2,1)S(1)} %get-tuple-element.332), channel_id=1, source_target_pairs={{0,1},{1,0},{2,3},{3,2},{4,5},{5,4},{6,7},{7,6},{8,9},{9,8},{10,11... | collective-permute-start | bytes 3145736 | tf_op jit(solution)/shard_map/ppermute | solution.py:234
  (93 other events, 1120.5 us)
